TPU v7x, 32 devices: a whole 2x2x4 slice. The times are simulated.
32 devices in a mesh: mod: 2 (over core), ctx: 4 (over z), dp: 4 (over y, x).
Axes of the slice: x: 2, y: 2, z: 4, core: 2. Of those that a mesh axis runs over, the one named last changes fastest.
Arguments:
- hidden_in: bfloat16 [4, 64, 4096], P('dp', ('mod', 'ctx')), may hold values from -6 to 6
- query_modality: int32 [4, 64], P('dp', ('mod', 'ctx')), may hold values from 0 to 1, as said below
- key_cache: bfloat16 [4, 8192, 4096], P('dp', None, 'ctx'), may hold values from -6 to 6
- value_cache: bfloat16 [4, 8192, 4096], P('dp', None, 'ctx'), may hold values from -6 to 6
- key_modality: int32 [4, 8192], P('dp'), may hold values from 0 to 1
- norm_attn: float32 [2, 4096], P('mod'), may hold values from 0.5 to 1.5
- query_weight: bfloat16 [2, 4096, 4096], P('mod', 'dp', 'ctx'), may hold values from -0.09375 to 0.09375
- query_gain: float32 [2, 4096], P('mod', 'ctx'), may hold values from 0.5 to 2.5
- key_gain: float32 [2, 4096], P(None, 'ctx'), may hold values from 0.5 to 2.5
- out_weight: bfloat16 [2, 4096, 4096], P('mod', 'ctx', 'dp'), may hold values from -0.09375 to 0.09375
- norm_ffn: float32 [2, 4096], P('mod'), may hold values from 0.5 to 1.5
- gate_weight: bfloat16 [2, 4096, 11008], P('mod', 'dp', 'ctx'), may hold values from -0.09375 to 0.09375
- up_weight: bfloat16 [2, 4096, 11008], P('mod', 'dp', 'ctx'), may hold values from -0.09375 to 0.09375
- down_weight: bfloat16 [2, 11008, 4096], P('mod', 'ctx', 'dp'), may hold values from -0.0546875 to 0.0546875
Outputs:
- mixed_out: bfloat16 [4, 64, 4096], P('dp', ('mod', 'ctx'))
Inputs may be any that keep to these rules, and one draw needn't show every extreme that they name: `query_modality`: each sequence has one main modality, drawn. The slab splits into aligned blocks of 8 tokens, one block a device; in each aligned pair of blocks (2j and 2j + 1) one block holds 6 tokens of the main modality and the other 4, the rest being the other modality, so a sequence's slab holds exactly 40 tokens of its main modality.
All inputs are finite; a program needn't handle non-finite values.
Results may differ from a plain program's by a relative error of at most 0.007.
Values may be sent and summed in bfloat16 or wider, within the bound.
A program may use at most 320 MiB of HBM per device.

v0:
```python
import math

import jax
import jax.numpy as jnp
from jax import lax
from jax.sharding import PartitionSpec as P

HD = 128


epsilon = 1e-05


def rms_scale(values, scales):
    inverse = lax.rsqrt(jnp.mean(values * values, axis=-1, keepdims=True) + epsilon)
    return values * inverse * scales


def slot_layout(all_ids, modality, rows_dev, n_ctx, n_mod):
    local_cap = 3 * rows_dev // 4
    slot_ids = jnp.arange(local_cap, dtype=jnp.int32)
    row_ids = jnp.arange(rows_dev, dtype=jnp.int32)
    targets = jnp.arange(n_mod, dtype=jnp.int32)
    block_ids = all_ids.reshape(n_mod, n_ctx, rows_dev).transpose(1, 0, 2)
    block_mask = block_ids == modality
    block_rank = jnp.cumsum(block_mask.astype(jnp.int32), axis=2) - 1
    block_hits = (block_rank[:, :, None, :] == slot_ids[None, None, :, None]) & block_mask[
        :, :, None, :
    ]
    local_pos = jnp.sum(block_hits.astype(jnp.int32) * row_ids[None, None, None, :], axis=3)
    is_valid = jnp.any(block_hits, axis=3).reshape(-1)
    block_base = (targets[None, :] * n_ctx + jnp.arange(n_ctx, dtype=jnp.int32)[:, None]) * rows_dev
    positions = (block_base[:, :, None] + local_pos).reshape(-1)
    return (positions, is_valid)


def gathered_rows(hidden_in, positions):
    whole_slab = lax.all_gather(hidden_in, ("mod", "ctx"), axis=1, tiled=True)[0]
    return whole_slab[positions]


def per_device(
    hidden_in,
    query_modality,
    key_cache,
    value_cache,
    key_modality,
    norm_attn,
    query_weight,
    query_gain,
    key_gain,
    out_weight,
    norm_ffn,
    gate_weight,
    up_weight,
    down_weight,
):
    modality = lax.axis_index("mod")
    ctx_index = lax.axis_index("ctx")
    n_ctx = lax.axis_size("ctx")
    n_mod = lax.axis_size("mod")
    rows_dev = hidden_in.shape[1]
    all_ids = lax.all_gather(query_modality, ("mod", "ctx"), axis=1, tiled=True)[0]
    slab_len = all_ids.shape[0]
    positions, is_valid = slot_layout(all_ids, modality, rows_dev, n_ctx, n_mod)
    row_block = gathered_rows(hidden_in, positions)
    q_weight, o_weight, g_weight, u_weight, d_weight = (
        lax.all_gather(query_weight, "dp", axis=1, tiled=True),
        lax.all_gather(out_weight, "dp", axis=2, tiled=True),
        lax.all_gather(gate_weight, "dp", axis=1, tiled=True),
        lax.all_gather(up_weight, "dp", axis=1, tiled=True),
        lax.all_gather(down_weight, "dp", axis=2, tiled=True),
    )
    q_weight = q_weight[0]
    o_weight = o_weight[0]
    g_weight = g_weight[0]
    u_weight = u_weight[0]
    d_weight = d_weight[0]
    head_dim = HD
    width_here = q_weight.shape[1]
    heads_here = width_here // head_dim
    cache_len = key_cache.shape[1]
    resid_rows = row_block.astype(jnp.float32)
    normed = rms_scale(resid_rows, norm_attn[0]).astype(jnp.bfloat16)
    projected = jnp.dot(normed, q_weight, preferred_element_type=jnp.float32).reshape(
        -1, heads_here, head_dim
    )
    query_heads = rms_scale(projected, query_gain[0].reshape(heads_here, head_dim)).astype(
        jnp.bfloat16
    )
    key_scale = jnp.where(
        key_modality[0][:, None] == 0, key_gain[0][None, :], key_gain[1][None, :]
    ).reshape(cache_len, heads_here, head_dim)
    key_heads = rms_scale(
        key_cache[0].astype(jnp.float32).reshape(cache_len, heads_here, head_dim), key_scale
    ).astype(jnp.bfloat16)
    value_heads = value_cache[0].reshape(cache_len, heads_here, head_dim)
    query_pos = cache_len - slab_len + positions
    scores = jnp.einsum(
        "nhe,che->hnc", query_heads, key_heads, preferred_element_type=jnp.float32
    ) * (1.0 / math.sqrt(head_dim))
    allowed = jnp.arange(cache_len, dtype=jnp.int32)[None, :] <= query_pos[:, None]
    scores = jnp.where(allowed[None, :, :], scores, -1e30)
    row_max = jnp.max(scores, axis=-1, keepdims=True)
    weights = jnp.exp(scores - row_max)
    row_total = jnp.sum(weights, axis=-1)
    summed = jnp.einsum(
        "hnc,che->nhe",
        weights.astype(jnp.bfloat16),
        value_heads,
        preferred_element_type=jnp.float32,
    )
    head_out = (summed / row_total.T[:, :, None]).astype(jnp.bfloat16).reshape(-1, width_here)
    partial_value = jnp.dot(head_out, o_weight, preferred_element_type=jnp.float32)
    share_rows = partial_value.shape[0] // n_ctx
    head_share = lax.psum_scatter(
        partial_value.astype(jnp.bfloat16), "ctx", scatter_dimension=0, tiled=True
    ).astype(jnp.float32)
    own_rows = lax.dynamic_slice_in_dim(resid_rows, ctx_index * share_rows, share_rows, 0)
    own_residual = own_rows + head_share
    normed_share = rms_scale(own_residual, norm_ffn[0]).astype(jnp.bfloat16)
    normed_ffn = lax.all_gather(normed_share, "ctx", axis=0, tiled=True)
    residual_term = lax.dynamic_update_slice_in_dim(
        jnp.zeros_like(partial_value), own_residual, ctx_index * share_rows, 0
    )
    gate_val = jnp.dot(normed_ffn, g_weight, preferred_element_type=jnp.float32)
    up_val = jnp.dot(normed_ffn, u_weight, preferred_element_type=jnp.float32)
    activated = (jax.nn.silu(gate_val) * up_val).astype(jnp.bfloat16)
    ffn_out = jnp.dot(activated, d_weight, preferred_element_type=jnp.float32)
    term_rows = jnp.where(is_valid[:, None], ffn_out + residual_term, 0.0)
    scatter_at = jnp.where(is_valid, positions, slab_len)
    full_term = (
        jnp.zeros((slab_len, ffn_out.shape[1]), jnp.float32)
        .at[scatter_at]
        .add(term_rows, mode="drop")
    )
    mixed_rows = lax.psum_scatter(full_term, ("mod", "ctx"), scatter_dimension=0, tiled=True)
    return mixed_rows.astype(jnp.bfloat16)[None]


def solution(mesh):
    placed = (
        P("dp", ("mod", "ctx"), None),
        P("dp", ("mod", "ctx")),
        P("dp", None, "ctx"),
        P("dp", None, "ctx"),
        P("dp", None),
        P("mod", None),
        P("mod", "dp", "ctx"),
        P("mod", "ctx"),
        P(None, "ctx"),
        P("mod", "ctx", "dp"),
        P("mod", None),
        P("mod", "dp", "ctx"),
        P("mod", "dp", "ctx"),
        P("mod", "ctx", "dp"),
    )
    return jax.shard_map(
        per_device,
        mesh=mesh,
        in_specs=placed,
        out_specs=P("dp", ("mod", "ctx"), None),
        check_vma=False,
    )
```

profile of v0, /device:TPU:0, one launch (start us, length us, event | category | flops | bytes accessed | tf_op | source)
XLA Modules:
  0.0 869.4 jit_solution(7280502352774455443)
XLA Ops:
  6.5 0.7 all-gather.7.cloned.1.call-update
  7.3 0.7 all-gather.9.cloned.1.call-update
  8.1 0.7 all-gather.11.cloned.1.call-update
  8.8 0.5 all-gather.13.cloned.1.call-update
  9.4 0.5 all-gather.15.cloned.1.call-update
  10.0 0.6 dynamic-slice.1
  11.3 10.7 %all-reduce = s32[64]{0:T(128)S(1)} all-reduce(s32[64]{0:T(128)S(1)} %bitcast_dynamic-update-slice_fusion), channel_id=1, replica_groups=mesh['mod'=2,'ctx'=4,'dp'=4] {'mod','ctx'}, use_global_device_ids=true, to_apply=%add | all-reduce | flops 64 | bytes 512
  22.2 0.4 reduce_window_sum.11
  22.6 0.3 select_reduce_fusion
  23.1 0.3 fusion.65
  23.4 0.1 copy.40
  23.8 18.6 %convert_bitcast_fusion = f32[1024,8,8,128]{3,1,2,0:T(8,128)} fusion(bf16[1,8192,1024]{2,1,0:T(8,128)(2,1)} %param.16), kind=kLoop, calls=%fused_computation.2 | loop fusion | flops 8388608 | bytes 50331648
  42.4 18.3 %copy.51 = f32[1024,8,8,128]{3,2,1,0:T(8,128)S(1)} copy(f32[1024,8,8,128]{3,1,2,0:T(8,128)} %convert_bitcast_fusion) | data formatting | bytes 67108864
  60.7 11.1 %copy-done.1 = f32[1024,8,8,128]{3,2,1,0:T(8,128)} copy-done((f32[1024,8,8,128]{3,2,1,0:T(8,128)}, f32[1024,8,8,128]{3,2,1,0:T(8,128)S(1)}, u32[]{:S(2)}) %copy-start.1) | copy-done | bytes 33554456
  71.8 15.8 %multiply_reduce_fusion = f32[8192,8]{1,0:T(8,128)} fusion(f32[8192,8,128]{2,1,0:T(8,128)S(1)} %bitcast.75), kind=kLoop, calls=%fused_computation.4 | loop fusion | flops 16711680 | bytes 33816576 | tf_op jit(solution)/shard_map/reduce_sum | solution.py:15
  87.6 2.8 copy.45
  90.4 2.6 copy.46
  93.0 15.9 %copy.52 = bf16[1024,8,8,128]{3,2,1,0:T(8,128)(2,1)} copy(bf16[1024,8,8,128]{3,1,2,0:T(8,128)(2,1)} %bitcast.79) | data formatting | bytes 33554432
  108.9 27.0 %all_gather.25 = bf16[1,64,4096]{2,1,0:T(8,128)(2,1)S(1)} all-gather(bf16[1,8,4096]{2,1,0:T(8,128)(2,1)S(1)} %copy-done.2), channel_id=1, replica_groups=mesh['mod'=2,'ctx'=4,'dp'=4] {'mod','ctx'}, dimensions={1}, use_global_device_ids=true | all-gather | bytes 589824 | tf_op jit(solution)/shard_map/all_gather | solution.py:38
  135.9 0.8 gather_fusion
  136.7 0.1 compare_reduce_fusion
  136.8 0.2 multiply_reduce_fusion.1
  137.0 0.3 iota_compare_fusion
  137.3 48.1 %multiply_convert_fusion = bf16[8192,8,128]{2,1,0:T(8,128)(2,1)} fusion(f32[8,128]{1,0:T(8,128)S(1)} %bitcast.84, f32[8,128]{1,0:T(8,128)S(1)} %bitcast.83, f32[8192,8]{1,0:T(8,128)} %copy.46, pred[8192]{0:T(1024)(128)(4,1)S(1)} %compare_reduce_fusion, f32[1024,8,8,128]{3,2,1,0:T(8,128)} %copy-done.1), kind=kLoop, calls=%fused_computation.3 | loop fusion | flops 33554432 | bytes 50610176 | tf_op jit(solution)/shard_map/convert_element_type | solution.py:96
  185.5 11.3 %copy.44 = bf16[1024,4096]{1,0:T(8,128)(2,1)} copy(bf16[1024,4096]{0,1:T(8,128)(2,1)} %bitcast.80) | data formatting | bytes 16777216 | tf_op jit(solution)/shard_map/dot_general | solution.py:85
  196.8 8.4 multiply_reduce_fusion.3
  205.2 17.7 %fusion.69 = (f32[8,48]{1,0:T(8,128)S(1)}, f32[8,48,8192]{2,1,0:T(8,128)}) fusion(bf16[8192,8,128]{2,1,0:T(8,128)(2,1)} %multiply_convert_fusion, f32[48,8,128]{2,0,1:T(8,128)S(1)} %get-tuple-element.12, f32[8,128]{1,0:T(8,128)S(1)} %bitcast.88, f32[48,8]{0,1:T(8,128)S(1)} %add_rsqrt_fusion.1, pred[48,8192]{1,0:T(8,128)(4,1)S(1)} %iota_compare_fusion), kind=kOutput, calls=%fused_computation.77 | convolution fusion | flops 814890624 | bytes 29957120 | tf_op jit(solution)/shard_map/nhe,che->hnc/dot_general | solution.py:99
  222.9 6.5 fusion.13
  229.4 1.6 copy-done
  231.1 12.2 %fusion.43 = bf16[8,6,8,128]{3,2,1,0:T(8,128)(2,1)S(1)} fusion(bf16[8192,8,128]{2,1,0:T(8,128)(2,1)} %bitcast.76, f32[8,48,8192]{2,1,0:T(8,128)S(1)} %copy-done, f32[8,48]{1,0:T(8,128)S(1)} %get-tuple-element.13, f32[48,8]{0,1:T(8,128)S(1)} %bitcast.81), kind=kOutput, calls=%fused_computation.29 | convolution fusion | flops 811696128 | bytes 29461504 | tf_op jit(solution)/shard_map/hnc,che->nhe/dot_general | solution.py:107
  243.4 4.9 fusion.19
  248.3 15.3 %fusion = bf16[16,4096]{1,0:T(8,128)(2,1)S(1)} fusion(bf16[48,4096]{1,0:T(8,128)(2,1)S(1)} %fusion.19), kind=kCustom, calls=%all-reduce-scatter | all-reduce-scatter fusion | flops 262145 | bytes 524800
  263.6 2.3 collective-permute-start
  266.1 0.6 dynamic-slice.6
  267.3 1.1 collective-permute-done
  268.4 0.3 concatenate
  268.7 0.2 multiply_reduce_fusion.2
  269.0 15.6 %all-gather = bf16[4,12,4096]{2,1,0:T(8,128)(2,1)S(1)} all-gather(bf16[1,12,4096]{2,1,0:T(8,128)(2,1)S(1)} %fusion.59), channel_id=1, replica_groups=mesh['mod'=2,'ctx'=4,'dp'=4] {'ctx'}, dimensions={0}, use_global_device_ids=true | all-gather | bytes 491520 | tf_op jit(solution)/shard_map/all_gather | solution.py:122
  284.7 112.0 %all-gather.11.cloned.1.call-done = bf16[1,4096,2752]{1,2,0:T(8,128)(2,1)} async-done(((bf16[1,1024,2752]{1,2,0:T(8,128)(2,1)}), bf16[1,4096,2752]{1,2,0:T(8,128)(2,1)}) %all-gather.11.cloned.1.call-update) | async-done | bytes 22544400 | tf_op jit(solution)/shard_map/all_gather | solution.py:70
  396.8 11.0 %fusion.5 = f32[48,2752]{1,0:T(8,128)S(1)} fusion(bf16[48,4096]{1,0:T(8,128)(2,1)S(1)} %reshape.217, bf16[1,4096,2752]{1,2,0:T(8,128)(2,1)} %all-gather.11.cloned.1.call-done), kind=kOutput, calls=%fused_computation.9 | convolution fusion | flops 1082130432 | bytes 23465984 | tf_op jit(solution)/shard_map/dot_general | solution.py:126
  407.8 196.7 %all-gather.13.cloned.1.call-done = bf16[1,4096,2752]{1,2,0:T(8,128)(2,1)} async-done(((bf16[1,1024,2752]{1,2,0:T(8,128)(2,1)}), bf16[1,4096,2752]{1,2,0:T(8,128)(2,1)}) %all-gather.13.cloned.1.call-update) | async-done | bytes 22544400 | tf_op jit(solution)/shard_map/all_gather | solution.py:71
  604.5 11.2 %fusion.25 = bf16[48,2752]{1,0:T(8,128)(2,1)S(1)} fusion(bf16[48,4096]{1,0:T(8,128)(2,1)S(1)} %reshape.217, bf16[1,4096,2752]{1,2,0:T(8,128)(2,1)} %all-gather.13.cloned.1.call-done, f32[48,2752]{1,0:T(8,128)S(1)} %fusion.5), kind=kOutput, calls=%fused_computation.24 | convolution fusion | flops 1082923008 | bytes 23730176 | tf_op jit(solution)/shard_map/dot_general | solution.py:127
  615.7 196.6 %all-gather.15.cloned.1.call-done = bf16[1,2752,4096]{2,1,0:T(8,128)(2,1)} async-done(((bf16[1,2752,1024]{2,1,0:T(8,128)(2,1)}), bf16[1,2752,4096]{2,1,0:T(8,128)(2,1)}) %all-gather.15.cloned.1.call-update) | async-done | bytes 22544400 | tf_op jit(solution)/shard_map/all_gather | solution.py:72
  812.3 9.5 %fusion.1 = f32[48,4096]{1,0:T(8,128)S(1)} fusion(bf16[48,2752]{1,0:T(8,128)(2,1)S(1)} %fusion.25, bf16[1,2752,4096]{2,1,0:T(8,128)(2,1)} %all-gather.15.cloned.1.call-done), kind=kOutput, calls=%fused_computation.5 | convolution fusion | flops 1082130432 | bytes 23595008 | tf_op jit(solution)/shard_map/dot_general | solution.py:129
  821.9 0.3 add.165
  822.2 2.7 scatter_custom_fusion
  824.9 36.1 %reduce-scatter.4.cloned.1.call-done = f32[8,4096]{1,0:T(8,128)} async-done(((f32[64,4096]{1,0:T(8,128)}), f32[8,4096]{1,0:T(8,128)}) %reduce-scatter.4.cloned.1.call-update) | async-done | bytes 131088 | tf_op jit(solution)/shard_map/reduce_scatter | solution.py:137
  861.0 1.5 convert_bitcast_fusion.1
  (56 shorter events, 1.6 us)
Async XLA Ops:
  6.5 3.4 copy-start.10
  6.5 4.7 copy-start.9
  6.5 178.9 %all-gather.7.cloned.1.call-start = ((), (), s32[]{:S(2)}) async-start(), calls=%async_computation.1 | async-start | bytes 10485760 | tf_op jit(solution)/shard_map/all_gather | solution.py:68
  7.3 236.1 %all-gather.9.cloned.1.call-start = ((), (), s32[]{:S(2)}) async-start(), calls=%async_computation.2 | async-start | bytes 10485760 | tf_op jit(solution)/shard_map/all_gather | solution.py:69
  8.0 388.8 %all-gather.11.cloned.1.call-start = ((), (), s32[]{:S(2)}) async-start(), calls=%async_computation.3 | async-start | bytes 28180480 | tf_op jit(solution)/shard_map/all_gather | solution.py:70
  8.7 595.8 %all-gather.13.cloned.1.call-start = ((), (), s32[]{:S(2)}) async-start(), calls=%async_computation.4 | async-start | bytes 28180480 | tf_op jit(solution)/shard_map/all_gather | solution.py:71
  9.3 803.0 %all-gather.15.cloned.1.call-start = ((), (), s32[]{:S(2)}) async-start(), calls=%async_computation.5 | async-start | bytes 28180480 | tf_op jit(solution)/shard_map/all_gather | solution.py:72
  9.9 851.1 %reduce-scatter.4.cloned.1.call-start = ((), (), s32[]{:S(2)}) async-start(), calls=%async_computation.6 | async-start | bytes 1179648 | tf_op jit(solution)/shard_map/reduce_scatter | solution.py:137
  60.7 11.1 %copy-start.1 = (f32[1024,8,8,128]{3,2,1,0:T(8,128)}, f32[1024,8,8,128]{3,2,1,0:T(8,128)S(1)}, u32[]{:S(2)}) copy-start(f32[1024,8,8,128]{3,2,1,0:T(8,128)S(1)} %copy.51) | copy-start | bytes 100663296
  93.0 15.9 %copy-start.2 = (bf16[1,8,4096]{2,1,0:T(8,128)(2,1)S(1)}, bf16[1,8,4096]{2,1,0:T(8,128)(2,1)}, u32[]{:S(2)}) copy-start(bf16[1,8,4096]{2,1,0:T(8,128)(2,1)} %param.14) | copy-start | bytes 196612
  93.0 43.7 %copy-start.3 = (s32[1,8192]{1,0:T(1,128)S(1)}, s32[1,8192]{1,0:T(1,128)}, u32[]{:S(2)}) copy-start(s32[1,8192]{1,0:T(1,128)} %param.18) | copy-start | bytes 98308
  93.0 44.0 %copy-start.6 = (f32[2,1024]{1,0:T(2,128)S(1)}, f32[2,1024]{1,0:T(2,128)}, u32[]{:S(2)}) copy-start(f32[2,1024]{1,0:T(2,128)} %param.22) | copy-start | bytes 24580
  185.4 11.3 %copy-start.4 = (f32[1,4096]{1,0:T(1,128)S(1)}, f32[1,4096]{1,0:T(1,128)}, u32[]{:S(2)}) copy-start(f32[1,4096]{1,0:T(1,128)} %param.19) | copy-start | bytes 49156
  185.5 19.7 %copy-start.8 = (f32[1,1024]{1,0:T(1,128)S(1)}, f32[1,1024]{1,0:T(1,128)}, u32[]{:S(2)}) copy-start(f32[1,1024]{1,0:T(1,128)} %param.21) | copy-start | bytes 12292
  222.9 8.2 copy-start
  243.3 22.7 %copy-start.7 = (u32[32]{0:T(128)S(1)}, u32[32]{0:T(128)}, u32[]{:S(2)}) copy-start(u32[32]{0:T(128)} %constant.86) | copy-start | bytes 388
  243.3 25.6 %copy-start.5 = (f32[1,4096]{1,0:T(1,128)S(1)}, f32[1,4096]{1,0:T(1,128)}, u32[]{:S(2)}) copy-start(f32[1,4096]{1,0:T(1,128)} %param.24) | copy-start | bytes 49156
  263.6 4.8 collective-permute-start
Sparse Core Ops, SparseCore 0:
  9.2 90.1 all-gather.6
  101.3 87.5 all-gather.8
  190.7 205.9 all-gather.10
  398.5 205.9 all-gather.12
  606.2 205.9 all-gather.14
  825.1 35.9 reduce-scatter.3
where the time goes:
time: 870 us; the launch traced here: 869 us
  waiting for transfers between devices  546 us (63%)
  other arithmetic  95.4 us (11%)
  matrix products  75 us (9%)
  blocking collectives  68.6 us (8%)
  local copies, waits for them, and re-layouts  67.1 us (8%)
  between operations  15.1 us (2%)
    all_gather x1, waiting for transfers between devices, per_device(): lax.all_gather(up_weight, 'dp', axis=1, tiled=True)  197 us
    all_gather x1, waiting for transfers between devices, per_device(): lax.all_gather(down_weight, 'dp', axis=2, tiled=True)  197 us
    all_gather x1, waiting for transfers between devices, per_device(): lax.all_gather(gate_weight, 'dp', axis=1, tiled=True)  112 us
    unnamed x31, local copies, waits for them, and re-layouts  48.6 us
    convert_element_type x1, other arithmetic, per_device(): key_heads = rms_scale(key_cache[0].astype(jnp.float32).reshape(cache_len,...  48.1 us
    reduce_scatter x1, waiting for transfers between devices, per_device(): lax.psum_scatter(full_term, ('mod', 'ctx'), scatter_dimension=0, tiled=True)  36.1 us
    all_gather x1, blocking collectives, gathered_rows(): lax.all_gather(hidden_in, ('mod', 'ctx'), axis=1, tiled=True)[0]  27 us
    unnamed x2, blocking collectives  26 us
  transfers between devices with their start and end apart: 7, of which 5 were waited for; matrix products, arithmetic and copies ran while one was open for 26% of the time, Pallas kernels for 0%

commit v1 on v0

v1 whole, which is shorter than its diff:
```python
import functools
import math

import jax
import jax.numpy as jnp
from jax import lax
from jax.experimental import pallas as pl
from jax.experimental.pallas import tpu as pltpu
from jax.sharding import PartitionSpec as P

HD = 128
LANES = 128

epsilon = 1e-05
bf16 = jnp.bfloat16
f32 = jnp.float32


def exchange_kernel(axis, n, gather, x_ref, o_ref, send_sems, recv_sems, own_sem):
    me = lax.axis_index(axis)
    barrier = pltpu.get_barrier_semaphore()
    for step in range(1, n):
        pl.semaphore_signal(
            barrier,
            inc=1,
            device_id={axis: lax.rem(me + step, n)},
            device_id_type=pl.DeviceIdType.MESH,
        )
    pl.semaphore_wait(barrier, n - 1)
    copies = []
    for step in range(1, n):
        peer = lax.rem(me + step, n)
        copy = pltpu.make_async_remote_copy(
            src_ref=x_ref if gather else x_ref.at[peer],
            dst_ref=o_ref.at[me],
            send_sem=send_sems.at[step],
            recv_sem=recv_sems.at[step],
            device_id={axis: peer},
            device_id_type=pl.DeviceIdType.MESH,
        )
        copy.start()
        copies.append(copy)
    own = pltpu.make_async_copy(x_ref if gather else x_ref.at[me], o_ref.at[me], own_sem)
    own.start()
    own.wait()
    for copy in copies:
        copy.wait()


def exchange(x, axis, call_id, gather=False):
    n = lax.axis_size(axis)
    shape = (n,) + x.shape if gather else x.shape
    return pl.pallas_call(
        functools.partial(exchange_kernel, axis, n, gather),
        out_shape=jax.ShapeDtypeStruct(shape, x.dtype),
        in_specs=[pl.BlockSpec(memory_space=pltpu.VMEM)],
        out_specs=pl.BlockSpec(memory_space=pltpu.VMEM),
        scratch_shapes=[
            pltpu.SemaphoreType.DMA((n,)),
            pltpu.SemaphoreType.DMA((n,)),
            pltpu.SemaphoreType.DMA,
        ],
        compiler_params=pltpu.CompilerParams(collective_id=call_id, has_side_effects=True),
        name=f"exchange_{call_id}_{axis}",
    )(x)


def attend_kernel(heads, rows, chunk, first_free, at_ref, q_ref, k_ref, v_ref, m_ref, o_ref, acc, total):
    step = pl.program_id(0)

    @pl.when(step == 0)
    def _():
        acc[...] = jnp.zeros_like(acc)
        total[...] = jnp.zeros_like(total)

    is_first = m_ref[...] == 0
    key_pos = step * chunk + lax.broadcasted_iota(jnp.int32, (rows, chunk), 1)
    row_pos = first_free + at_ref[1] + lax.broadcasted_iota(jnp.int32, (rows, chunk), 0)
    allowed = key_pos <= row_pos
    ones = jnp.ones((8, HD), bf16)
    over_width = (((1,), (1,)), ((), ()))
    for head in range(heads):
        cut = slice(head * HD, (head + 1) * HD)
        keys = k_ref[:, cut]
        both = lax.dot_general(q_ref[head], keys, over_width, preferred_element_type=f32)
        wide = keys.astype(f32)
        squares = lax.dot_general(
            ones, (wide * wide).astype(bf16), over_width, preferred_element_type=f32
        )[:1]
        inverse = lax.rsqrt(squares * (1.0 / HD) + epsilon)
        scores = jnp.where(is_first, both[:rows], both[rows:]) * inverse
        probs = jnp.where(allowed, jnp.exp(scores), 0.0)
        total[head] += jnp.sum(probs, axis=1, keepdims=True)
        acc[head] += jnp.dot(probs.astype(bf16), v_ref[:, cut], preferred_element_type=f32)

    @pl.when(step == pl.num_programs(0) - 1)
    def _():
        for head in range(heads):
            o_ref[:, head * HD : (head + 1) * HD] = (acc[head] / total[head]).astype(bf16)


def attend(queries, key_cache, value_cache, key_modality, column, row_start, slab_len):
    heads, double, _ = queries.shape
    rows = double // 2
    cache_len = key_cache.shape[0]
    chunk = min(1024, cache_len)
    width = heads * HD
    where_at = jnp.stack([column, row_start]).astype(jnp.int32)
    return pl.pallas_call(
        functools.partial(attend_kernel, heads, rows, chunk, cache_len - slab_len),
        out_shape=jax.ShapeDtypeStruct((rows, width), bf16),
        grid_spec=pltpu.PrefetchScalarGridSpec(
            num_scalar_prefetch=1,
            grid=(cache_len // chunk,),
            in_specs=[
                pl.BlockSpec((heads, double, HD), lambda j, at: (0, 0, 0)),
                pl.BlockSpec((chunk, width), lambda j, at: (j, at[0])),
                pl.BlockSpec((chunk, width), lambda j, at: (j, at[0])),
                pl.BlockSpec((1, chunk), lambda j, at: (0, j)),
            ],
            out_specs=pl.BlockSpec((rows, width), lambda j, at: (0, 0)),
            scratch_shapes=[
                pltpu.VMEM((heads, rows, HD), f32),
                pltpu.VMEM((heads, rows, 1), f32),
            ],
        ),
        compiler_params=pltpu.CompilerParams(dimension_semantics=("arbitrary",)),
        name="attend",
    )(where_at, queries, key_cache, value_cache, key_modality)


def two_parts(values):
    high = values.astype(bf16)
    return high, (values - high.astype(f32)).astype(bf16)


def beside(values, columns):
    extra = jnp.stack([c.astype(bf16) for c in columns], axis=-1)
    pad = [(0, 0)] * (extra.ndim - 1) + [(0, LANES - extra.shape[-1])]
    return jnp.concatenate([values.astype(bf16), jnp.pad(extra, pad)], axis=-1)


def per_device(
    hidden_in,
    query_modality,
    key_cache,
    value_cache,
    key_modality,
    norm_attn,
    query_weight,
    query_gain,
    key_gain,
    out_weight,
    norm_ffn,
    gate_weight,
    up_weight,
    down_weight,
):
    m = lax.axis_index("mod")
    d = lax.axis_index("dp")
    n_mod, n_ctx, n_dp = lax.axis_size("mod"), lax.axis_size("ctx"), lax.axis_size("dp")
    rows, model = hidden_in.shape[1:]
    part = model // n_dp
    width = query_weight.shape[2]
    hidden_units = gate_weight.shape[2]
    heads = width // HD
    slab_len = n_mod * n_ctx * rows
    by_heads = heads % n_mod == 0

    hidden = hidden_in[0]
    wide = hidden.astype(f32)
    inverse = lax.rsqrt(jnp.mean(wide * wide, axis=-1) + epsilon)
    sent = jnp.broadcast_to(
        beside(jnp.zeros((rows, 0), bf16), (query_modality[0], *two_parts(inverse)))[None],
        (n_dp, rows, LANES),
    )
    pieces = hidden.reshape(rows, n_dp, part).transpose(1, 0, 2)
    own_block = exchange(jnp.concatenate([pieces, sent], axis=-1), "dp", 0)
    slab = exchange(own_block, "ctx", 1, gather=True)
    slab = exchange(slab, "mod", 2, gather=True)
    tags = slab[..., part : part + 3].astype(f32)
    ids = tags[..., 0]
    is_mine = ids == m.astype(f32)

    gain = lax.dynamic_slice_in_dim(norm_attn[0], d * part, part)
    row_inverse = (tags[..., 1] + tags[..., 2])[..., None]
    normed = jnp.where(
        is_mine[..., None], slab[..., :part].astype(f32) * row_inverse * gain, 0.0
    ).astype(bf16)
    tokens = n_dp * slab_len
    projected = jnp.dot(
        normed.reshape(tokens, part), query_weight[0], preferred_element_type=f32
    ).astype(bf16)
    gains = jnp.pad(jnp.stack(two_parts(query_gain[0])), ((0, 14), (0, 0)))
    if by_heads:
        to_mod = (
            jnp.concatenate([projected, gains], axis=0)
            .reshape(tokens + 16, n_mod, width // n_mod)
            .transpose(1, 0, 2)
        )
    else:
        to_mod = jnp.concatenate(
            [
                projected.reshape(n_mod, tokens // n_mod, width),
                jnp.broadcast_to(gains[None], (n_mod, 16, width)),
            ],
            axis=1,
        )
    from_mod = exchange(to_mod, "mod", 3).astype(f32)
    split_width = from_mod.shape[-1]
    both_gains = from_mod[:, -16] + from_mod[:, -15]
    blocks = n_ctx * n_mod if by_heads else n_ctx
    to_dp = (
        jnp.sum(from_mod[:, :-16], axis=0)
        .astype(bf16)
        .reshape(blocks, n_dp, rows, split_width)
        .transpose(1, 0, 2, 3)
        .reshape(n_dp, blocks * rows, split_width)
    )
    projected = jnp.sum(exchange(to_dp, "dp", 4).astype(f32), axis=0)
    count = blocks * rows
    split_heads = split_width // HD
    own_ids = lax.dynamic_index_in_dim(ids, d, 2, keepdims=False)
    if by_heads:
        own_ids = own_ids.reshape(count)
        column, row_start = m, jnp.int32(0)
        key_gains = lax.dynamic_slice_in_dim(key_gain, m * split_width, split_width, 1)
    else:
        own_ids = lax.dynamic_index_in_dim(own_ids, m, 0, keepdims=False).reshape(count)
        column, row_start = jnp.int32(0), m * count
        key_gains = key_gain
    token_gain = jnp.where(own_ids[:, None] == 0, both_gains[0][None], both_gains[1][None])
    by_head = projected.reshape(count, split_heads, HD)
    by_head = by_head * lax.rsqrt(
        jnp.mean(by_head * by_head, axis=-1, keepdims=True) + epsilon
    )
    by_head = by_head * token_gain.reshape(count, split_heads, HD) * (1.0 / math.sqrt(HD))
    queries = by_head[None] * key_gains.reshape(2, 1, split_heads, HD)
    queries = (
        queries.astype(bf16).transpose(2, 0, 1, 3).reshape(split_heads, 2 * count, HD)
    )
    head_out = attend(
        queries, key_cache[0], value_cache[0], key_modality, column, row_start, slab_len
    )

    shared = exchange(head_out, "dp", 5, gather=True)
    shared = exchange(shared, "mod", 6, gather=True)
    if by_heads:
        shared = shared.transpose(1, 2, 0, 3).reshape(n_dp, n_mod, n_ctx * rows, width)
        shared = shared.transpose(1, 0, 2, 3)
    ids_mdcr = is_mine.transpose(0, 2, 1, 3).reshape(n_mod, n_dp, n_ctx * rows, 1)

    def to_blocks(values, weight, first_id):
        masked = jnp.where(ids_mdcr, values, jnp.zeros_like(values))
        product = jnp.dot(
            masked.reshape(tokens, values.shape[-1]), weight, preferred_element_type=f32
        ).astype(bf16)
        product = product.reshape(n_mod, n_dp * n_ctx * rows, part)
        product = exchange(product, "mod", first_id).astype(f32)
        product = (
            jnp.sum(product, axis=0)
            .astype(bf16)
            .reshape(n_dp, n_ctx, rows, part)
            .transpose(1, 0, 2, 3)
        )
        return jnp.sum(exchange(product, "ctx", first_id + 1).astype(f32), axis=0)

    attention = to_blocks(shared, out_weight[0], 7)
    residual = own_block[..., :part].astype(f32) + attention
    squares = jnp.sum(residual * residual, axis=-1)

    slab = exchange(beside(residual, two_parts(squares)), "ctx", 9, gather=True)
    slab = exchange(slab, "mod", 10, gather=True)
    gain = lax.dynamic_slice_in_dim(norm_ffn[0], d * part, part)
    scaled = jnp.where(is_mine[..., None], slab[..., :part].astype(f32) * gain, 0.0)
    scaled = scaled.astype(bf16).reshape(tokens, part)
    gate = jnp.dot(scaled, gate_weight[0], preferred_element_type=f32).astype(bf16)
    up = jnp.dot(scaled, up_weight[0], preferred_element_type=f32).astype(bf16)

    def over_mod(values, call_id):
        values = values.reshape(n_mod, tokens // n_mod, hidden_units)
        values = jnp.sum(exchange(values, "mod", call_id).astype(f32), axis=0).astype(bf16)
        values = values.reshape(n_ctx, n_dp, rows, hidden_units).transpose(1, 0, 2, 3)
        return values.reshape(n_dp, n_ctx * rows, hidden_units)

    own_squares = lax.dynamic_index_in_dim(slab[..., part : part + 2], m, 0, keepdims=False)
    own_squares = own_squares.transpose(1, 0, 2, 3).reshape(n_dp, n_ctx * rows, 2)
    own_squares = jnp.pad(own_squares, ((0, 0), (0, 0), (0, LANES - 2)))
    to_dp = jnp.concatenate([over_mod(gate, 11), own_squares], axis=-1)
    gate = jnp.sum(exchange(to_dp, "dp", 12).astype(f32), axis=0)
    up = jnp.sum(exchange(over_mod(up, 13), "dp", 14).astype(f32), axis=0)
    squares = gate[:, hidden_units : hidden_units + 1] + gate[:, hidden_units + 1 : hidden_units + 2]
    inverse = lax.rsqrt(squares * (1.0 / model) + epsilon)
    activated = (jax.nn.silu(gate[:, :hidden_units] * inverse) * (up * inverse)).astype(bf16)
    shared = exchange(activated, "dp", 15, gather=True)
    shared = exchange(shared, "mod", 16, gather=True)
    mixed = residual + to_blocks(shared, down_weight[0], 17)
    home = exchange(mixed.astype(bf16), "dp", 19)
    return home.transpose(1, 0, 2).reshape(1, rows, model)


def solution(mesh):
    placed = (
        P("dp", ("mod", "ctx"), None),
        P("dp", ("mod", "ctx")),
        P("dp", None, "ctx"),
        P("dp", None, "ctx"),
        P("dp", None),
        P("mod", None),
        P("mod", "dp", "ctx"),
        P("mod", "ctx"),
        P(None, "ctx"),
        P("mod", "ctx", "dp"),
        P("mod", None),
        P("mod", "dp", "ctx"),
        P("mod", "dp", "ctx"),
        P("mod", "ctx", "dp"),
    )
    return jax.shard_map(
        per_device,
        mesh=mesh,
        in_specs=placed,
        out_specs=P("dp", ("mod", "ctx"), None),
        check_vma=False,
    )
```

time: 870 us -> 224 us (0.26)
  waiting for transfers between devices: 546 us -> 0 us
  Pallas kernels: 0 us -> 163 us
  blocking collectives: 68.6 us -> 0 us
  other arithmetic: 95.4 us -> 27.7 us
  matrix products: 75 us -> 15.8 us
  local copies, waits for them, and re-layouts: 67.1 us -> 15.3 us
  between operations: 15.1 us -> 0.4 us
    all_gather x5 -> x0, waiting for transfers between devices: 505 us -> none  [the longest x1 197 us: per_device(): lax.all_gather(up_weight, 'dp', axis=1, tiled=True)]
    pallas_call x0 -> x21, Pallas kernels: none -> 163 us  [the longest x20 147 us: exchange(): pl.pallas_call(functools.partial(exchange_kernel, axis, n, gather), out_s...]
    dot_general x7 -> x5, matrix products: 75 us -> 15.8 us  [the longest x2 6.54 us: to_blocks(): jnp.dot(masked.reshape(tokens, values.shape[-1]), weight, preferred_eleme...]
    unnamed x31 -> x10, local copies, waits for them, and re-layouts: 48.6 us -> 3.01 us
    all_gather x2 -> x0, blocking collectives: 42.6 us -> none  [the longest x1 27 us: gathered_rows(): lax.all_gather(hidden_in, ('mod', 'ctx'), axis=1, tiled=True)[0]]
    convert_element_type x3 -> x13, other arithmetic: 48.2 us -> 8.31 us  [the longest x1 1.33 us: per_device(): normed = jnp.where(is_mine[..., None], slab[..., :part].astype(f32) * row...]
    reduce_scatter x1 -> x0, waiting for transfers between devices: 36.1 us -> none  [per_device(): lax.psum_scatter(full_term, ('mod', 'ctx'), scatter_dimension=0, tiled=True)]
    unnamed x2 -> x0, blocking collectives: 26 us -> none
  transfers between devices with their start and end apart: 7 -> 0, of which waited for: 5 -> 0; matrix products, arithmetic and copies ran while one was open for 26% -> 0% of each run, Pallas kernels for 0% -> 0%
where the time goes in v1:
time: 224 us; the launch traced here: 222 us
  Pallas kernels  163 us (73%)
  other arithmetic  27.7 us (12%)
  matrix products  15.8 us (7%)
  local copies, waits for them, and re-layouts  15.3 us (7%)
    pallas_call x20, Pallas kernels, exchange(): pl.pallas_call(functools.partial(exchange_kernel, axis, n, gather), out_s...  147 us
    pallas_call x1, Pallas kernels, attend(): pl.pallas_call(functools.partial(attend_kernel, heads, rows, chunk, cache...  15.4 us
    dot_general x2, matrix products, to_blocks(): jnp.dot(masked.reshape(tokens, values.shape[-1]), weight, preferred_eleme...  6.54 us

profile of v1, /device:TPU:0, one launch (start us, length us, event | category | flops | bytes accessed | tf_op | source)
XLA Modules:
  0.0 222.1 jit_solution(16977337360621125467)
XLA Ops:
  0.0 1.1 multiply_reduce_fusion.2
  4.7 1.5 pad_maximum_fusion.1.x_ref
  6.2 8.0 %exchange_0_dp.1.x_ref = bf16[4,8,1152]{2,1,0:T(8,128)(2,1)} custom-call(bf16[4,8,1152]{2,1,0:T(8,128)(2,1)} %pad_maximum_fusion.1.x_ref), custom_call_target="tpu_custom_call" | custom-call | tf_op jit(solution)/shard_map/exchange_0_dp/pallas_call | solution.py:53
  14.2 10.5 %exchange_1_ctx.1.x_ref = bf16[4,4,8,1152]{3,2,1,0:T(8,128)(2,1)} custom-call(bf16[4,8,1152]{2,1,0:T(8,128)(2,1)} %exchange_0_dp.1.x_ref), custom_call_target="tpu_custom_call" | custom-call | tf_op jit(solution)/shard_map/exchange_1_ctx/pallas_call | solution.py:53
  24.7 3.4 %exchange_2_mod.1 = bf16[2,4,4,8,1152]{4,3,2,1,0:T(8,128)(2,1)} custom-call(bf16[4,4,8,1152]{3,2,1,0:T(8,128)(2,1)} %exchange_1_ctx.1.x_ref), custom_call_target="tpu_custom_call" | custom-call | tf_op jit(solution)/shard_map/exchange_2_mod/pallas_call | solution.py:53
  30.0 1.3 select_convert_fusion.1
  33.2 3.5 %exchange_3_mod.1 = bf16[2,272,512]{2,1,0:T(8,128)(2,1)} custom-call(bf16[2,272,512]{2,1,0:T(8,128)(2,1)} %bitcast.123), custom_call_target="tpu_custom_call" | custom-call | tf_op jit(solution)/shard_map/exchange_3_mod/pallas_call | solution.py:53
  36.7 1.2 convert_element_type.207
  38.7 8.2 %exchange_4_dp.1 = bf16[4,64,512]{2,1,0:T(8,128)(2,1)} custom-call(bf16[4,64,512]{2,1,0:T(8,128)(2,1)} %bitcast.127), custom_call_target="tpu_custom_call" | custom-call | tf_op jit(solution)/shard_map/exchange_4_dp/pallas_call | solution.py:53
  46.9 1.0 convert_reduce_fusion.4
  49.0 15.4 %attend.1.x_ref = bf16[64,512]{1,0:T(8,128)(2,1)} custom-call(s32[2]{0:T(128)} %pad_add_fusion.at_ref, bf16[4,128,128]{2,1,0:T(8,128)(2,1)} %bitcast.132, bf16[8192,1024]{1,0:T(8,128)(2,1)} %bitcast.114, bf16[8192,1024]{1,0:T(8,128)(2,1)} %bitcast.115, s32[1,8192]{1,0:T(1,128)} %m_ref.1), custom_call_target="tpu_custom_call" | custom-call | tf_op jit(solution)/shard_map/attend/pallas_call | solution.py:109
  64.4 7.9 %exchange_5_dp.1.x_ref = bf16[4,64,512]{2,1,0:T(8,128)(2,1)} custom-call(bf16[64,512]{1,0:T(8,128)(2,1)} %attend.1.x_ref), custom_call_target="tpu_custom_call" | custom-call | tf_op jit(solution)/shard_map/exchange_5_dp/pallas_call | solution.py:53
  72.3 3.3 %exchange_6_mod.1 = bf16[2,4,64,512]{3,2,1,0:T(8,128)(2,1)} custom-call(bf16[4,64,512]{2,1,0:T(8,128)(2,1)} %exchange_5_dp.1.x_ref), custom_call_target="tpu_custom_call" | custom-call | tf_op jit(solution)/shard_map/exchange_6_mod/pallas_call | solution.py:53
  75.7 1.6 copy.98
  77.8 1.4 copy-done.3
  79.2 1.5 fusion.20
  80.7 3.5 %exchange_7_mod.1 = bf16[2,128,1024]{2,1,0:T(8,128)(2,1)} custom-call(bf16[2,128,1024]{2,1,0:T(8,128)(2,1)} %bitcast.137), custom_call_target="tpu_custom_call" | custom-call | tf_op jit(solution)/shard_map/exchange_7_mod/pallas_call | solution.py:53
  84.2 1.1 reduce_sum.135
  86.1 10.6 %exchange_8_ctx.1 = bf16[4,4,8,1024]{3,2,1,0:T(8,128)(2,1)} custom-call(bf16[4,4,8,1024]{3,2,1,0:T(8,128)(2,1)} %bitcast.128), custom_call_target="tpu_custom_call" | custom-call | tf_op jit(solution)/shard_map/exchange_8_ctx/pallas_call | solution.py:53
  96.6 1.0 convert_reduce_fusion.3
  98.5 11.2 %exchange_9_ctx.1.x_ref = bf16[4,4,8,1152]{3,2,1,0:T(8,128)(2,1)} custom-call(bf16[4,8,1152]{2,1,0:T(8,128)(2,1)} %fusion.29.x_ref), custom_call_target="tpu_custom_call" | custom-call | tf_op jit(solution)/shard_map/exchange_9_ctx/pallas_call | solution.py:53
  109.7 3.4 %exchange_10_mod.1 = bf16[2,4,4,8,1152]{4,3,2,1,0:T(8,128)(2,1)} custom-call(bf16[4,4,8,1152]{3,2,1,0:T(8,128)(2,1)} %exchange_9_ctx.1.x_ref), custom_call_target="tpu_custom_call" | custom-call | tf_op jit(solution)/shard_map/exchange_10_mod/pallas_call | solution.py:53
  113.9 1.2 select_convert_fusion
  115.5 4.3 %fusion.9 = bf16[256,2752]{0,1:T(8,128)(2,1)S(1)} fusion(bf16[256,1024]{1,0:T(8,128)(2,1)S(1)} %bitcast.133, bf16[1,1024,2752]{1,2,0:T(8,128)(2,1)} %param.26), kind=kOutput, calls=%fused_computation.7 | convolution fusion | flops 1443545088 | bytes 7569408 | tf_op jit(solution)/shard_map/dot_general | solution.py:278
  119.8 1.7 copy.106
  121.5 4.7 %exchange_13_mod.1 = bf16[2,128,2752]{2,1,0:T(8,128)(2,1)} custom-call(bf16[2,128,2752]{2,1,0:T(8,128)(2,1)} %bitcast.116), custom_call_target="tpu_custom_call" | custom-call | tf_op jit(solution)/shard_map/exchange_13_mod/pallas_call | solution.py:53
  126.2 1.7 reduce_sum.141
  127.9 0.9 copy.118
  128.8 13.0 %exchange_14_dp.1 = bf16[4,32,2752]{2,1,0:T(8,128)(2,1)} custom-call(bf16[4,32,2752]{2,1,0:T(8,128)(2,1)} %bitcast.121), custom_call_target="tpu_custom_call" | custom-call | tf_op jit(solution)/shard_map/exchange_14_dp/pallas_call | solution.py:53
  141.8 1.2 convert_reduce_fusion.1
  143.1 4.3 %fusion.6 = bf16[256,2752]{0,1:T(8,128)(2,1)S(1)} fusion(bf16[256,1024]{1,0:T(8,128)(2,1)S(1)} %bitcast.134, bf16[1,1024,2752]{1,2,0:T(8,128)(2,1)} %param.25), kind=kOutput, calls=%fused_computation.6 | convolution fusion | flops 1443545088 | bytes 7569408 | tf_op jit(solution)/shard_map/dot_general | solution.py:277
  147.3 1.7 copy.102
  149.0 4.7 %exchange_11_mod.1 = bf16[2,128,2752]{2,1,0:T(8,128)(2,1)} custom-call(bf16[2,128,2752]{2,1,0:T(8,128)(2,1)} %bitcast.117), custom_call_target="tpu_custom_call" | custom-call | tf_op jit(solution)/shard_map/exchange_11_mod/pallas_call | solution.py:53
  153.7 1.7 reduce_sum.139
  155.5 1.0 fusion.26.x_ref
  156.5 13.8 %exchange_12_dp.1 = bf16[4,32,2880]{2,1,0:T(8,128)(2,1)} custom-call(bf16[4,32,2880]{2,1,0:T(8,128)(2,1)} %fusion.26.x_ref), custom_call_target="tpu_custom_call" | custom-call | tf_op jit(solution)/shard_map/exchange_12_dp/pallas_call | solution.py:53
  170.3 1.3 convert_reduce_fusion
  171.7 0.9 multiply_convert_fusion.x_ref
  172.6 13.1 %exchange_15_dp.1.x_ref = bf16[4,32,2752]{2,1,0:T(8,128)(2,1)} custom-call(bf16[32,2752]{1,0:T(8,128)(2,1)} %multiply_convert_fusion.x_ref), custom_call_target="tpu_custom_call" | custom-call | tf_op jit(solution)/shard_map/exchange_15_dp/pallas_call | solution.py:53
  185.7 4.5 %exchange_16_mod.1 = bf16[2,4,32,2752]{3,2,1,0:T(8,128)(2,1)} custom-call(bf16[4,32,2752]{2,1,0:T(8,128)(2,1)} %exchange_15_dp.1.x_ref), custom_call_target="tpu_custom_call" | custom-call | tf_op jit(solution)/shard_map/exchange_16_mod/pallas_call | solution.py:53
  190.2 1.5 broadcast_select_fusion
  191.7 5.0 %fusion.23 = bf16[256,1024]{1,0:T(8,128)(2,1)} fusion(bf16[256,2752]{1,0:T(8,128)(2,1)S(1)} %bitcast.125, bf16[1,2752,1024]{2,1,0:T(8,128)(2,1)} %param.27), kind=kOutput, calls=%fused_computation.19 | convolution fusion | flops 1443102720 | bytes 7569408 | tf_op jit(solution)/shard_map/dot_general | solution.py:255
  196.7 3.6 %exchange_17_mod.1 = bf16[2,128,1024]{2,1,0:T(8,128)(2,1)} custom-call(bf16[2,128,1024]{2,1,0:T(8,128)(2,1)} %bitcast.138), custom_call_target="tpu_custom_call" | custom-call | tf_op jit(solution)/shard_map/exchange_17_mod/pallas_call | solution.py:53
  200.3 1.1 reduce_sum.143
  202.2 10.6 %exchange_18_ctx.1 = bf16[4,4,8,1024]{3,2,1,0:T(8,128)(2,1)} custom-call(bf16[4,4,8,1024]{3,2,1,0:T(8,128)(2,1)} %bitcast.129), custom_call_target="tpu_custom_call" | custom-call | tf_op jit(solution)/shard_map/exchange_18_ctx/pallas_call | solution.py:53
  212.8 1.0 convert_reduce_fusion.2
  214.4 6.2 %exchange_19_dp.1 = bf16[4,8,1024]{2,1,0:T(8,128)(2,1)} custom-call(bf16[4,8,1024]{2,1,0:T(8,128)(2,1)} %add_convert_fusion.x_ref), custom_call_target="tpu_custom_call" | custom-call | tf_op jit(solution)/shard_map/exchange_19_dp/pallas_call | solution.py:53
  220.6 1.5 copy.125
  (57 shorter events, 14.1 us)
Async XLA Ops:
  0.0 31.6 %copy-start = (bf16[1,1024,1024]{2,1,0:T(8,128)(2,1)S(1)}, bf16[1,1024,1024]{2,1,0:T(8,128)(2,1)}, u32[]{:S(2)}) copy-start(bf16[1,1024,1024]{2,1,0:T(8,128)(2,1)} %param.20) | copy-start | bytes 6291460
  77.6 1.6 copy-start.3
  80.7 16.9 %copy-start.2 = (bf16[4,8,1152]{2,1,0:T(8,128)(2,1)S(1)}, bf16[4,8,1152]{2,1,0:T(8,128)(2,1)}, u32[]{:S(2)}) copy-start(bf16[4,8,1152]{2,1,0:T(8,128)(2,1)} %exchange_0_dp.1.x_ref) | copy-start | bytes 221188
  196.7 25.4 %copy-start.1 = (bf16[1,1024,1024]{2,1,0:T(8,128)(2,1)S(1)}, bf16[1,1024,1024]{2,1,0:T(8,128)(2,1)}, u32[]{:S(2)}) copy-start(bf16[1,1024,1024]{2,1,0:T(8,128)(2,1)} %param.20) | copy-start | bytes 6291460

commit v2 on v1

v2 whole, which is shorter than its diff:
```python
import functools
import math

import jax
import jax.numpy as jnp
from jax import lax
from jax.experimental import pallas as pl
from jax.experimental.pallas import tpu as pltpu
from jax.sharding import PartitionSpec as P

HD = 128
LANES = 128

epsilon = 1e-05
bf16 = jnp.bfloat16
f32 = jnp.float32


def greet(axes):
    barrier = pltpu.get_barrier_semaphore()
    count = 0
    for axis in axes:
        me, n = lax.axis_index(axis), lax.axis_size(axis)
        for step in range(1, n):
            pl.semaphore_signal(
                barrier,
                inc=1,
                device_id={axis: lax.rem(me + step, n)},
                device_id_type=pl.DeviceIdType.MESH,
            )
        count += n - 1
    pl.semaphore_wait(barrier, count)


def send(source, target, sems, slot, axis, peer):
    copy = pltpu.make_async_remote_copy(
        src_ref=source,
        dst_ref=target,
        send_sem=sems[0].at[slot],
        recv_sem=sems[1].at[slot],
        device_id={axis: peer},
        device_id_type=pl.DeviceIdType.MESH,
    )
    copy.start()
    return copy


def copy_here(source, target, sem):
    copy = pltpu.make_async_copy(source, target, sem)
    copy.start()
    copy.wait()


def swap_all(axis, source_of, target_of, sems, own_sem):
    me, n = lax.axis_index(axis), lax.axis_size(axis)
    copies = []
    for step in range(1, n):
        peer = lax.rem(me + step, n)
        copies.append(send(source_of(peer), target_of(me), sems, step, axis, peer))
    copy_here(source_of(me), target_of(me), own_sem)
    for copy in copies:
        copy.wait()


def spread(axis, source, place, sems, relay_sems, own_sem):
    me, n = lax.axis_index(axis), lax.axis_size(axis)
    m, n_mod = lax.axis_index("mod"), lax.axis_size("mod")
    copies, relays = [], []
    for step in range(1, n):
        peer = lax.rem(me + step, n)
        copies.append(send(source, place(m, me), sems, step, axis, peer))

    def relay(block, origin, step):
        for other in range(1, n_mod):
            partner = lax.rem(m + other, n_mod)
            slot = (other - 1) * n + step
            relays.append(send(block, place(m, origin), relay_sems, slot, "mod", partner))

    relay(source, me, 0)
    copy_here(source, place(m, me), own_sem)
    for step in range(1, n):
        copies[step - 1].wait_recv()
        origin = lax.rem(me + n - step, n)
        relay(place(m, origin), origin, step)
    for copy in copies:
        copy.wait_send()
    for copy in relays:
        copy.wait()


def dma_sems(*counts):
    return [pltpu.SemaphoreType.DMA((count,)) for count in counts for _ in range(2)]


def communicate(kernel, call_id, name, operands, outs, scratch):
    whole = pl.BlockSpec(memory_space=pltpu.VMEM)
    return pl.pallas_call(
        kernel,
        out_shape=outs,
        in_specs=[whole] * len(operands),
        out_specs=[whole] * len(outs),
        scratch_shapes=scratch,
        compiler_params=pltpu.CompilerParams(
            collective_id=call_id, has_side_effects=True, vmem_limit_bytes=60 * 2**20
        ),
        name=name,
    )(*operands)


def enter_kernel(x_ref, block_ref, o_ref, s0, r0, s1, r1, s2, r2, own_sem):
    greet(("dp", "ctx", "mod"))
    swap_all("dp", lambda i: x_ref.at[i], lambda i: block_ref.at[i], (s0, r0), own_sem)
    spread("ctx", block_ref, lambda j, i: o_ref.at[:, j, i], (s1, r1), (s2, r2), own_sem)


def enter(x, call_id):
    n_dp, rows, cols = x.shape
    n_mod, n_ctx = lax.axis_size("mod"), lax.axis_size("ctx")
    return communicate(
        enter_kernel,
        call_id,
        "enter",
        (x,),
        [
            jax.ShapeDtypeStruct(x.shape, x.dtype),
            jax.ShapeDtypeStruct((n_dp, n_mod, n_ctx, rows, cols), x.dtype),
        ],
        dma_sems(n_dp, n_ctx, n_mod * n_ctx) + [pltpu.SemaphoreType.DMA],
    )


def gather(x, axis, shape, place, call_id):
    n_mod, n = lax.axis_size("mod"), lax.axis_size(axis)

    def kernel(x_ref, o_ref, s1, r1, s2, r2, own_sem):
        greet((axis, "mod"))
        spread(axis, x_ref, lambda j, i: place(o_ref, j, i), (s1, r1), (s2, r2), own_sem)

    return communicate(
        kernel,
        call_id,
        f"gather_{call_id}_{axis}",
        (x,),
        [jax.ShapeDtypeStruct(shape, x.dtype)],
        dma_sems(n, n_mod * n) + [pltpu.SemaphoreType.DMA],
    )[0]


def home_kernel(x_ref, o_ref, s0, r0, own_sem):
    greet(("dp",))
    swap_all("dp", lambda i: x_ref.at[i], lambda i: o_ref.at[i], (s0, r0), own_sem)


def to_home(x, call_id):
    return communicate(
        home_kernel,
        call_id,
        "to_home",
        (x,),
        [jax.ShapeDtypeStruct(x.shape, x.dtype)],
        dma_sems(x.shape[0]) + [pltpu.SemaphoreType.DMA],
    )[0]


def reduce_kernel(axis, count, block, *refs):
    me, n = lax.axis_index(axis), lax.axis_size(axis)
    m, n_mod = lax.axis_index("mod"), lax.axis_size("mod")
    xs, outs = refs[:count], refs[count : 2 * count]
    near, far, land = (refs[(2 + i) * count : (3 + i) * count] for i in range(3))
    s1, r1, s2, r2 = refs[5 * count :]
    greet((axis, "mod"))
    order = list(range(1, n)) + [0]
    swaps, copies = {}, []
    for step in order:
        peer = lax.rem(me + step, n)
        for which in range(count):
            for other in range(1, n_mod):
                partner = lax.rem(m + other, n_mod)
                slot = ((other - 1) * n + step) * count + which
                swaps[step, which, other] = send(
                    block(xs[which], partner, peer),
                    near[which].at[other - 1, step],
                    (s1, r1),
                    slot,
                    "mod",
                    partner,
                )

    def over_mod(step, which):
        total = block(xs[which], m, lax.rem(me + step, n))[...].astype(f32)
        for other in range(1, n_mod):
            swaps[step, which, other].wait_recv()
            total += near[which][other - 1, step].astype(f32)
        return total

    for step in range(1, n):
        for which in range(count):
            far[which][step] = over_mod(step, which).astype(bf16)
            copies.append(
                send(
                    far[which].at[step],
                    land[which].at[step],
                    (s2, r2),
                    step * count + which,
                    axis,
                    lax.rem(me + step, n),
                )
            )
    for which in range(count):
        outs[which][...] = over_mod(0, which)
    for index, copy in enumerate(copies):
        copy.wait_recv()
        step, which = 1 + index // count, index % count
        outs[which][...] += land[which][step].astype(f32)
    for copy in copies:
        copy.wait_send()
    for copy in swaps.values():
        copy.wait_send()


def reduce(xs, axis, block, block_shapes, call_id):
    n_mod, n, count = lax.axis_size("mod"), lax.axis_size(axis), len(xs)
    slots = [pltpu.VMEM((n_mod - 1, n) + shape, bf16) for shape in block_shapes]
    lines = [pltpu.VMEM((n,) + shape, bf16) for shape in block_shapes]
    return communicate(
        functools.partial(reduce_kernel, axis, count, block),
        call_id,
        f"reduce_{call_id}_{axis}",
        xs,
        [jax.ShapeDtypeStruct(shape, f32) for shape in block_shapes],
        slots + lines + lines + dma_sems(n_mod * n * count, n * count),
    )


def attend_kernel(heads, rows, chunk, first_free, at_ref, q_ref, k_ref, v_ref, m_ref, o_ref, acc, total):
    step = pl.program_id(0)

    @pl.when(step == 0)
    def _():
        acc[...] = jnp.zeros_like(acc)
        total[...] = jnp.zeros_like(total)

    ones = jnp.ones((8, HD), bf16)
    over_width = (((1,), (1,)), ((), ()))

    def add_chunk(masked):
        is_first = m_ref[...] == 0
        for head in range(heads):
            cut = slice(head * HD, (head + 1) * HD)
            keys = k_ref[:, cut]
            both = lax.dot_general(q_ref[head], keys, over_width, preferred_element_type=f32)
            wide = keys.astype(f32)
            squares = lax.dot_general(
                ones, (wide * wide).astype(bf16), over_width, preferred_element_type=f32
            )[:1]
            inverse = lax.rsqrt(squares * (1.0 / HD) + epsilon)
            probs = jnp.exp(jnp.where(is_first, both[:rows], both[rows:]) * inverse)
            if masked:
                key_pos = step * chunk + lax.broadcasted_iota(jnp.int32, (rows, chunk), 1)
                row_pos = lax.broadcasted_iota(jnp.int32, (rows, chunk), 0)
                probs = jnp.where(key_pos <= first_free + at_ref[1] + row_pos, probs, 0.0)
            total[head] += jnp.sum(probs, axis=1, keepdims=True)
            acc[head] += jnp.dot(probs.astype(bf16), v_ref[:, cut], preferred_element_type=f32)

    has_free = (step + 1) * chunk > first_free

    @pl.when(has_free)
    def _():
        add_chunk(True)

    @pl.when(jnp.logical_not(has_free))
    def _():
        add_chunk(False)

    @pl.when(step == pl.num_programs(0) - 1)
    def _():
        for head in range(heads):
            o_ref[:, head * HD : (head + 1) * HD] = (acc[head] / total[head]).astype(bf16)


def attend(queries, key_cache, value_cache, key_modality, column, row_start, slab_len):
    heads, double, _ = queries.shape
    rows = double // 2
    cache_len = key_cache.shape[0]
    chunk = min(1024, cache_len)
    width = heads * HD
    where_at = jnp.stack([column, row_start]).astype(jnp.int32)
    return pl.pallas_call(
        functools.partial(attend_kernel, heads, rows, chunk, cache_len - slab_len),
        out_shape=jax.ShapeDtypeStruct((rows, width), bf16),
        grid_spec=pltpu.PrefetchScalarGridSpec(
            num_scalar_prefetch=1,
            grid=(cache_len // chunk,),
            in_specs=[
                pl.BlockSpec((heads, double, HD), lambda j, at: (0, 0, 0)),
                pl.BlockSpec((chunk, width), lambda j, at: (j, at[0])),
                pl.BlockSpec((chunk, width), lambda j, at: (j, at[0])),
                pl.BlockSpec((1, chunk), lambda j, at: (0, j)),
            ],
            out_specs=pl.BlockSpec((rows, width), lambda j, at: (0, 0)),
            scratch_shapes=[
                pltpu.VMEM((heads, rows, HD), f32),
                pltpu.VMEM((heads, rows, 1), f32),
            ],
        ),
        compiler_params=pltpu.CompilerParams(dimension_semantics=("arbitrary",)),
        name="attend",
    )(where_at, queries, key_cache, value_cache, key_modality)


def two_parts(values):
    high = values.astype(bf16)
    return high, (values - high.astype(f32)).astype(bf16)


def beside(values, columns):
    extra = jnp.stack([c.astype(bf16) for c in columns], axis=-1)
    pad = [(0, 0)] * (extra.ndim - 1) + [(0, LANES - extra.shape[-1])]
    return jnp.concatenate([values.astype(bf16), jnp.pad(extra, pad)], axis=-1)


def per_device(
    hidden_in,
    query_modality,
    key_cache,
    value_cache,
    key_modality,
    norm_attn,
    query_weight,
    query_gain,
    key_gain,
    out_weight,
    norm_ffn,
    gate_weight,
    up_weight,
    down_weight,
):
    m = lax.axis_index("mod")
    d = lax.axis_index("dp")
    n_mod, n_ctx, n_dp = lax.axis_size("mod"), lax.axis_size("ctx"), lax.axis_size("dp")
    rows, model = hidden_in.shape[1:]
    part = model // n_dp
    width = query_weight.shape[2]
    hidden_units = gate_weight.shape[2]
    heads = width // HD
    slab_len = n_mod * n_ctx * rows
    by_heads = heads % n_mod == 0

    hidden = hidden_in[0]
    wide = hidden.astype(f32)
    inverse = lax.rsqrt(jnp.mean(wide * wide, axis=-1) + epsilon)
    sent = jnp.broadcast_to(
        beside(jnp.zeros((rows, 0), bf16), (query_modality[0], *two_parts(inverse)))[None],
        (n_dp, rows, LANES),
    )
    pieces = hidden.reshape(rows, n_dp, part).transpose(1, 0, 2)
    own_block, slab = enter(jnp.concatenate([pieces, sent], axis=-1), 0)
    tags = slab[..., part : part + 3].astype(f32)
    ids = tags[..., 0]
    is_mine = ids == m.astype(f32)

    gain = lax.dynamic_slice_in_dim(norm_attn[0], d * part, part)
    row_inverse = (tags[..., 1] + tags[..., 2])[..., None]
    normed = jnp.where(
        is_mine[..., None], slab[..., :part].astype(f32) * row_inverse * gain, 0.0
    ).astype(bf16)
    tokens = n_dp * slab_len
    projected = jnp.dot(
        normed.reshape(tokens, part), query_weight[0], preferred_element_type=f32
    ).astype(bf16)
    gains = jnp.stack(two_parts(query_gain[0]))
    gains = jnp.where(jnp.arange(n_mod)[:, None, None] == m, gains[None], jnp.zeros_like(gains)[None])
    gains = jnp.pad(gains.reshape(2 * n_mod, width), ((0, 16 - 2 * n_mod), (0, 0)))
    gains = jnp.where(d == 0, gains, jnp.zeros_like(gains))
    split_width = width // n_mod if by_heads else width
    blocks = n_ctx * n_mod if by_heads else n_ctx
    count = blocks * rows
    if by_heads:
        to_sum = jnp.concatenate(
            [
                projected.reshape(n_dp, count, width),
                jnp.broadcast_to(gains[None], (n_dp, 16, width)),
            ],
            axis=1,
        )
        to_sum = to_sum.reshape(n_dp, count + 16, n_mod, split_width).transpose(0, 2, 1, 3)
    else:
        to_sum = jnp.concatenate(
            [
                projected.reshape(n_dp, n_mod, count, width),
                jnp.broadcast_to(gains[None, None], (n_dp, n_mod, 16, width)),
            ],
            axis=2,
        )
    (summed,) = reduce(
        (to_sum,), "dp", lambda ref, j, i: ref.at[i, j], [(count + 16, split_width)], 1
    )
    projected = summed[:count]
    both_gains = summed[count : count + 2 * n_mod : 2] + summed[count + 1 : count + 2 * n_mod : 2]
    split_heads = split_width // HD
    own_ids = lax.dynamic_index_in_dim(ids, d, 0, keepdims=False)
    if by_heads:
        own_ids = own_ids.reshape(count)
        column, row_start = m, jnp.int32(0)
        key_gains = lax.dynamic_slice_in_dim(key_gain, m * split_width, split_width, 1)
    else:
        own_ids = lax.dynamic_index_in_dim(own_ids, m, 0, keepdims=False).reshape(count)
        column, row_start = jnp.int32(0), m * count
        key_gains = key_gain
    token_gain = jnp.where(own_ids[:, None] == 0, both_gains[0][None], both_gains[1][None])
    by_head = projected.reshape(count, split_heads, HD)
    by_head = by_head * lax.rsqrt(
        jnp.mean(by_head * by_head, axis=-1, keepdims=True) + epsilon
    )
    by_head = by_head * token_gain.reshape(count, split_heads, HD) * (1.0 / math.sqrt(HD))
    queries = by_head[None] * key_gains.reshape(2, 1, split_heads, HD)
    queries = (
        queries.astype(bf16).transpose(2, 0, 1, 3).reshape(split_heads, 2 * count, HD)
    )
    head_out = attend(
        queries, key_cache[0], value_cache[0], key_modality, column, row_start, slab_len
    )

    if by_heads:
        shared = gather(
            head_out,
            "dp",
            (n_dp, count, width),
            lambda ref, j, i: ref.at[i, :, pl.ds(pl.multiple_of(j * split_width, LANES), split_width)],
            2,
        )
    else:
        shared = gather(
            head_out, "dp", (n_dp, n_mod, count, width), lambda ref, j, i: ref.at[i, j], 2
        )

    def to_blocks(values, weight, call_id):
        values = values.reshape(tokens, values.shape[-1])
        masked = jnp.where(is_mine.reshape(tokens, 1), values, jnp.zeros_like(values))
        product = jnp.dot(masked, weight, preferred_element_type=f32).astype(bf16)
        product = product.reshape(n_dp, n_mod, n_ctx, rows, part)
        return reduce(
            (product,), "ctx", lambda ref, j, i: ref.at[:, j, i], [(n_dp, rows, part)], call_id
        )[0]

    attention = to_blocks(shared, out_weight[0], 3)
    residual = own_block[..., :part].astype(f32) + attention
    squares = jnp.sum(residual * residual, axis=-1)

    slab = gather(
        beside(residual, two_parts(squares)),
        "ctx",
        (n_dp, n_mod, n_ctx, rows, part + LANES),
        lambda ref, j, i: ref.at[:, j, i],
        4,
    )
    gain = lax.dynamic_slice_in_dim(norm_ffn[0], d * part, part)
    scaled = jnp.where(is_mine[..., None], slab[..., :part].astype(f32) * gain, 0.0)
    scaled = scaled.astype(bf16).reshape(tokens, part)
    by_block = (n_dp, n_mod, n_ctx * rows)
    gate = jnp.dot(scaled, gate_weight[0], preferred_element_type=f32).astype(bf16)
    up = jnp.dot(scaled, up_weight[0], preferred_element_type=f32).astype(bf16)
    squares = jnp.where(is_mine[..., None], slab[..., part:], jnp.zeros_like(slab[..., part:]))
    gate, up, squares = reduce(
        (
            gate.reshape(*by_block, hidden_units),
            up.reshape(*by_block, hidden_units),
            squares.reshape(*by_block, LANES),
        ),
        "dp",
        lambda ref, j, i: ref.at[i, j],
        [(n_ctx * rows, hidden_units)] * 2 + [(n_ctx * rows, LANES)],
        5,
    )
    inverse = lax.rsqrt((squares[:, :1] + squares[:, 1:2]) * (1.0 / model) + epsilon)
    activated = (jax.nn.silu(gate * inverse) * (up * inverse)).astype(bf16)
    shared = gather(
        activated, "dp", (*by_block, hidden_units), lambda ref, j, i: ref.at[i, j], 6
    )
    mixed = residual + to_blocks(shared, down_weight[0], 7)
    home = to_home(mixed.astype(bf16), 8)
    return home.transpose(1, 0, 2).reshape(1, rows, model)


def solution(mesh):
    placed = (
        P("dp", ("mod", "ctx"), None),
        P("dp", ("mod", "ctx")),
        P("dp", None, "ctx"),
        P("dp", None, "ctx"),
        P("dp", None),
        P("mod", None),
        P("mod", "dp", "ctx"),
        P("mod", "ctx"),
        P(None, "ctx"),
        P("mod", "ctx", "dp"),
        P("mod", None),
        P("mod", "dp", "ctx"),
        P("mod", "dp", "ctx"),
        P("mod", "ctx", "dp"),
    )
    return jax.shard_map(
        per_device,
        mesh=mesh,
        in_specs=placed,
        out_specs=P("dp", ("mod", "ctx"), None),
        check_vma=False,
    )
```

time: 224 us -> 185 us (0.83)
  Pallas kernels: 163 us -> 134 us
  other arithmetic: 27.7 us -> 21.6 us
  local copies, waits for them, and re-layouts: 15.3 us -> 9.85 us
    pallas_call x20 -> x9, Pallas kernels: 147 us -> 119 us  [communicate(): pl.pallas_call(kernel, out_shape=outs, in_specs=[whole] * len(operands),...]
    reduce_sum x10 -> x0, other arithmetic: 11.2 us -> none  [the longest x2 3.35 us: over_mod(): jnp.sum(exchange(values, 'mod', call_id).astype(f32), axis=0).astype(bf16)]
    transpose x6 -> x0, local copies, waits for them, and re-layouts: 3.45 us -> none  [the longest x1 1.58 us: per_device(): shared.transpose(1, 2, 0, 3).reshape(n_dp, n_mod, n_ctx * rows, width)]
    reshape x4 -> x0, local copies, waits for them, and re-layouts: 2.62 us -> none  [the longest x2 1.42 us: to_blocks(): product = jnp.sum(product, axis=0).astype(bf16).reshape(n_dp, n_ctx, rows...]
where the time goes in v2:
time: 185 us; the launch traced here: 184 us
  Pallas kernels  134 us (72%)
  other arithmetic  21.6 us (12%)
  matrix products  17.7 us (10%)
  local copies, waits for them, and re-layouts  9.85 us (5%)
    pallas_call x9, Pallas kernels, communicate(): pl.pallas_call(kernel, out_shape=outs, in_specs=[whole] * len(operands),...  119 us
    pallas_call x1, Pallas kernels, attend(): pl.pallas_call(functools.partial(attend_kernel, heads, rows, chunk, cache...  15.2 us
    dot_general x2, matrix products, to_blocks(): product = jnp.dot(masked, weight, preferred_element_type=f32).astype(bf16)  8.42 us
    dot_general x1, matrix products, per_device(): up = jnp.dot(scaled, up_weight[0], preferred_element_type=f32).astype(bf16)  4.26 us
    dot_general x1, matrix products, per_device(): jnp.dot(scaled, gate_weight[0], preferred_element_type=f32).astype(bf16)  4.26 us

profile of v2, /device:TPU:0, one launch (start us, length us, event | category | flops | bytes accessed | tf_op | source)
XLA Modules:
  0.0 183.8 jit_solution(9205965614904111253)
XLA Ops:
  0.0 1.1 multiply_reduce_fusion.2
  1.2 0.7 convert_bitcast_fusion
  1.8 0.6 pad_add_fusion.at_ref
  2.8 0.7 dynamic-slice_bitcast_fusion
  3.5 0.7 constant_dynamic-slice_fusion
  4.2 0.8 fusion.34
  5.1 1.5 pad_maximum_fusion.x_ref
  6.6 17.7 %enter.1 = (bf16[4,8,1152]{2,1,0:T(8,128)(2,1)}, bf16[4,2,4,8,1152]{4,3,2,1,0:T(8,128)(2,1)}) custom-call(bf16[4,8,1152]{2,1,0:T(8,128)(2,1)} %pad_maximum_fusion.x_ref), custom_call_target="tpu_custom_call" | custom-call | tf_op jit(solution)/shard_map/enter/pallas_call | solution.py:97
  24.3 0.9 slice_convert_fusion
  25.1 0.6 compare_reduce_fusion
  25.9 0.3 fusion.32
  26.2 1.3 select_convert_fusion.1
  27.5 0.2 fusion.29
  27.9 0.7 fusion.16
  28.6 0.4 concatenate.13
  29.0 0.9 maximum_bitcast_fusion.refs_0_
  29.9 10.2 %reduce_1_dp.1 = f32[80,512]{1,0:T(8,128)} custom-call(bf16[4,2,80,512]{3,2,1,0:T(8,128)(2,1)} %maximum_bitcast_fusion.refs_0_), custom_call_target="tpu_custom_call" | custom-call | tf_op jit(solution)/shard_map/reduce_1_dp/pallas_call | solution.py:97
  40.2 0.7 slice.53
  40.9 0.7 slice.52
  41.6 0.9 slice.51
  42.6 0.1 multiply_reduce_fusion.1
  42.8 0.2 multiply_bitcast_fusion
  43.0 0.7 multiply_convert_fusion.1
  43.7 15.2 %attend.1.x_ref = bf16[64,512]{1,0:T(8,128)(2,1)} custom-call(s32[2]{0:T(128)} %pad_add_fusion.at_ref, bf16[4,128,128]{2,1,0:T(8,128)(2,1)} %bitcast.86, bf16[8192,1024]{1,0:T(8,128)(2,1)} %bitcast.81, bf16[8192,1024]{1,0:T(8,128)(2,1)} %bitcast.82, s32[1,8192]{1,0:T(1,128)} %m_ref.1), custom_call_target="tpu_custom_call" | custom-call | tf_op jit(solution)/shard_map/attend/pallas_call | solution.py:288
  58.8 9.0 %gather_2_dp.1 = bf16[4,64,1024]{2,1,0:T(8,128)(2,1)} custom-call(bf16[64,512]{1,0:T(8,128)(2,1)} %attend.1.x_ref), custom_call_target="tpu_custom_call" | custom-call | tf_op jit(solution)/shard_map/gather_2_dp/pallas_call | solution.py:97
  67.9 1.1 broadcast_select_fusion.1
  69.1 3.1 %fusion.19 = bf16[256,1024]{1,0:T(8,128)(2,1)} fusion(bf16[256,1024]{1,0:T(8,128)(2,1)S(1)} %bitcast.92, bf16[1,1024,1024]{2,1,0:T(8,128)(2,1)} %param.23), kind=kOutput, calls=%fused_computation.14 | convolution fusion | flops 537133056 | bytes 3145728 | tf_op jit(solution)/shard_map/dot_general | solution.py:440
  72.2 12.1 %reduce_3_ctx.1 = f32[4,8,1024]{2,1,0:T(8,128)} custom-call(bf16[4,2,4,8,1024]{4,3,2,1,0:T(8,128)(2,1)} %bitcast.87), custom_call_target="tpu_custom_call" | custom-call | tf_op jit(solution)/shard_map/reduce_3_ctx/pallas_call | solution.py:97
  84.3 1.0 fusion.28
  85.3 0.1 copy.58
  85.5 0.6 fusion.27.x_ref
  86.1 12.8 %gather_4_ctx.1 = bf16[4,2,4,8,1152]{4,3,2,1,0:T(8,128)(2,1)} custom-call(bf16[4,8,1152]{2,1,0:T(8,128)(2,1)} %fusion.27.x_ref), custom_call_target="tpu_custom_call" | custom-call | tf_op jit(solution)/shard_map/gather_4_ctx/pallas_call | solution.py:97
  98.9 1.6 select_bitcast_fusion.refs_2_
  100.4 1.2 select_convert_fusion
  101.7 4.3 %fusion.9 = bf16[256,2752]{0,1:T(8,128)(2,1)S(1)} fusion(bf16[256,1024]{1,0:T(8,128)(2,1)S(1)} %bitcast.90, bf16[1,1024,2752]{1,2,0:T(8,128)(2,1)} %param.26), kind=kOutput, calls=%fused_computation.7 | convolution fusion | flops 1443545088 | bytes 7569408 | tf_op jit(solution)/shard_map/dot_general | solution.py:462
  105.9 1.7 copy.60
  107.6 4.3 %fusion.6 = bf16[256,2752]{0,1:T(8,128)(2,1)S(1)} fusion(bf16[256,1024]{1,0:T(8,128)(2,1)S(1)} %bitcast.91, bf16[1,1024,2752]{1,2,0:T(8,128)(2,1)} %param.25), kind=kOutput, calls=%fused_computation.6 | convolution fusion | flops 1443545088 | bytes 7569408 | tf_op jit(solution)/shard_map/dot_general | solution.py:461
  111.9 1.7 copy.59
  113.6 24.5 %reduce_5_dp.1 = (f32[32,2752]{1,0:T(8,128)}, f32[32,2752]{1,0:T(8,128)}, f32[32,128]{1,0:T(8,128)}) custom-call(bf16[4,2,32,2752]{3,2,1,0:T(8,128)(2,1)} %bitcast.84, bf16[4,2,32,2752]{3,2,1,0:T(8,128)(2,1)} %bitcast.83, bf16[4,2,32,128]{3,2,1,0:T(8,128)(2,1)} %select_bitcast_fusion.refs_2_), custom_call_target="tpu_custom_call" | custom-call | tf_op jit(solution)/shard_map/reduce_5_dp/pallas_call | solution.py:97
  138.1 1.0 rsqrt_reduce_fusion
  139.0 1.9 %multiply_convert_fusion.x_ref = bf16[32,2752]{1,0:T(8,128)(2,1)} fusion(f32[32,2752]{1,0:T(8,128)} %get-tuple-element.14, f32[32,2752]{1,0:T(8,128)} %get-tuple-element.12, f32[32]{0:T(128)S(1)} %rsqrt_reduce_fusion), kind=kLoop, calls=%fused_computation.20 | loop fusion | flops 704512 | bytes 880768 | tf_op jit(solution)/shard_map/convert_element_type | solution.py:476
  141.0 14.5 %gather_6_dp.1 = bf16[4,2,32,2752]{3,2,1,0:T(8,128)(2,1)} custom-call(bf16[32,2752]{1,0:T(8,128)(2,1)} %multiply_convert_fusion.x_ref), custom_call_target="tpu_custom_call" | custom-call | tf_op jit(solution)/shard_map/gather_6_dp/pallas_call | solution.py:97
  155.5 1.5 broadcast_select_fusion
  157.0 5.3 %fusion.22 = bf16[256,1024]{1,0:T(8,128)(2,1)} fusion(bf16[256,2752]{1,0:T(8,128)(2,1)S(1)} %bitcast.85, bf16[1,2752,1024]{2,1,0:T(8,128)(2,1)} %param.27), kind=kOutput, calls=%fused_computation.15 | convolution fusion | flops 1443102720 | bytes 7569408 | tf_op jit(solution)/shard_map/dot_general | solution.py:440
  162.3 12.3 %reduce_7_ctx.1 = f32[4,8,1024]{2,1,0:T(8,128)} custom-call(bf16[4,2,4,8,1024]{4,3,2,1,0:T(8,128)(2,1)} %bitcast.88), custom_call_target="tpu_custom_call" | custom-call | tf_op jit(solution)/shard_map/reduce_7_ctx/pallas_call | solution.py:97
  174.6 1.6 add_convert_fusion.x_ref
  176.2 6.2 %to_home.1 = bf16[4,8,1024]{2,1,0:T(8,128)(2,1)} custom-call(bf16[4,8,1024]{2,1,0:T(8,128)(2,1)} %add_convert_fusion.x_ref), custom_call_target="tpu_custom_call" | custom-call | tf_op jit(solution)/shard_map/to_home/pallas_call | solution.py:97
  182.3 1.5 copy.68
  (35 shorter events, 0.9 us)
Async XLA Ops:
  0.0 27.8 %copy-start = (bf16[1,1024,1024]{2,1,0:T(8,128)(2,1)S(1)}, bf16[1,1024,1024]{2,1,0:T(8,128)(2,1)}, u32[]{:S(2)}) copy-start(bf16[1,1024,1024]{2,1,0:T(8,128)(2,1)} %param.20) | copy-start | bytes 6291460
  69.0 15.3 %copy-start.3 = (bf16[4,8,1152]{2,1,0:T(8,128)(2,1)S(1)}, bf16[4,8,1152]{2,1,0:T(8,128)(2,1)}, u32[]{:S(2)}) copy-start(bf16[4,8,1152]{2,1,0:T(8,128)(2,1)} %get-tuple-element.10) | copy-start | bytes 221188
  157.0 17.6 %copy-start.2 = (f32[4,8,1024]{2,1,0:T(8,128)S(1)}, f32[4,8,1024]{2,1,0:T(8,128)}, u32[]{:S(2)}) copy-start(f32[4,8,1024]{2,1,0:T(8,128)} %reduce_3_ctx.1) | copy-start | bytes 393220
  157.0 26.8 %copy-start.1 = (bf16[1,1024,1024]{2,1,0:T(8,128)(2,1)S(1)}, bf16[1,1024,1024]{2,1,0:T(8,128)(2,1)}, u32[]{:S(2)}) copy-start(bf16[1,1024,1024]{2,1,0:T(8,128)(2,1)} %param.20) | copy-start | bytes 6291460

commit v3 on v2

--- a/solution.py
+++ b/solution.py
@@ -146,29 +146,17 @@
     )[0]
 
 
-def home_kernel(x_ref, o_ref, s0, r0, own_sem):
-    greet(("dp",))
-    swap_all("dp", lambda i: x_ref.at[i], lambda i: o_ref.at[i], (s0, r0), own_sem)
-
-
-def to_home(x, call_id):
-    return communicate(
-        home_kernel,
-        call_id,
-        "to_home",
-        (x,),
-        [jax.ShapeDtypeStruct(x.shape, x.dtype)],
-        dma_sems(x.shape[0]) + [pltpu.SemaphoreType.DMA],
-    )[0]
-
-
 def reduce_kernel(axis, count, block, *refs):
+    xs, outs = refs[:count], refs[count : 2 * count]
+    greet((axis, "mod"))
+    add_up(axis, count, block, xs, outs, *refs[2 * count :])
+
+
+def add_up(axis, count, block, xs, outs, *refs):
     me, n = lax.axis_index(axis), lax.axis_size(axis)
     m, n_mod = lax.axis_index("mod"), lax.axis_size("mod")
-    xs, outs = refs[:count], refs[count : 2 * count]
-    near, far, land = (refs[(2 + i) * count : (3 + i) * count] for i in range(3))
-    s1, r1, s2, r2 = refs[5 * count :]
-    greet((axis, "mod"))
+    near, far, land = (refs[i * count : (1 + i) * count] for i in range(3))
+    s1, r1, s2, r2 = refs[3 * count :]
     order = list(range(1, n)) + [0]
     swaps, copies = {}, []
     for step in order:
@@ -218,49 +206,128 @@
         copy.wait_send()
 
 
-def reduce(xs, axis, block, block_shapes, call_id):
-    n_mod, n, count = lax.axis_size("mod"), lax.axis_size(axis), len(xs)
+def add_up_scratch(axis, block_shapes):
+    n_mod, n, count = lax.axis_size("mod"), lax.axis_size(axis), len(block_shapes)
     slots = [pltpu.VMEM((n_mod - 1, n) + shape, bf16) for shape in block_shapes]
     lines = [pltpu.VMEM((n,) + shape, bf16) for shape in block_shapes]
+    return slots + lines + lines + dma_sems(n_mod * n * count, n * count)
+
+
+def reduce(xs, axis, block, block_shapes, call_id):
+    count = len(xs)
     return communicate(
         functools.partial(reduce_kernel, axis, count, block),
         call_id,
         f"reduce_{call_id}_{axis}",
         xs,
         [jax.ShapeDtypeStruct(shape, f32) for shape in block_shapes],
-        slots + lines + lines + dma_sems(n_mod * n * count, n * count),
-    )
-
-
-def attend_kernel(heads, rows, chunk, first_free, at_ref, q_ref, k_ref, v_ref, m_ref, o_ref, acc, total):
+        add_up_scratch(axis, block_shapes),
+    )
+
+
+def block_of_ctx(ref, j, i):
+    return ref.at[:, j, i]
+
+
+def renew_kernel(part, x_ref, own_ref, sum_ref, o_ref, message, *refs):
+    s1, r1, s2, r2, own_sem = refs[-5:]
+    greet(("ctx", "mod"))
+    add_up("ctx", 1, block_of_ctx, (x_ref,), (sum_ref,), *refs[:-5])
+    residual = sum_ref[...] + own_ref[:, :, :part].astype(f32)
+    sum_ref[...] = residual
+    message[:, :, :part] = residual.astype(bf16)
+    squares = jnp.sum(residual * residual, axis=-1, keepdims=True)
+    high, low = two_parts(squares)
+    lane = lax.broadcasted_iota(jnp.int32, squares.shape[:2] + (LANES,), 2)
+    tags = jnp.where(lane == 0, high.astype(f32), jnp.where(lane == 1, low.astype(f32), 0.0))
+    message[:, :, part:] = tags.astype(bf16)
+    spread("ctx", message, lambda j, i: block_of_ctx(o_ref, j, i), (s1, r1), (s2, r2), own_sem)
+
+
+def renew(product, own_block, call_id):
+    n_dp, n_mod, n_ctx, rows, part = product.shape
+    return communicate(
+        functools.partial(renew_kernel, part),
+        call_id,
+        "renew",
+        (product, own_block),
+        [
+            jax.ShapeDtypeStruct((n_dp, rows, part), f32),
+            jax.ShapeDtypeStruct((n_dp, n_mod, n_ctx, rows, part + LANES), bf16),
+        ],
+        [pltpu.VMEM((n_dp, rows, part + LANES), bf16)]
+        + add_up_scratch("ctx", [(n_dp, rows, part)])
+        + dma_sems(n_ctx, n_mod * n_ctx)
+        + [pltpu.SemaphoreType.DMA],
+    )
+
+
+def leave_kernel(part, x_ref, residual_ref, o_ref, total, message, *refs):
+    s0, r0, own_sem = refs[-3:]
+    greet(("ctx", "mod", "dp"))
+    add_up("ctx", 1, block_of_ctx, (x_ref,), (total,), *refs[:-3])
+    message[...] = (total[...] + residual_ref[...]).astype(bf16)
+
+    def share(i):
+        return o_ref.at[:, pl.ds(pl.multiple_of(i * part, part), part)]
+
+    swap_all("dp", lambda i: message.at[i], share, (s0, r0), own_sem)
+
+
+def leave(product, residual, call_id):
+    n_dp, n_mod, n_ctx, rows, part = product.shape
+    return communicate(
+        functools.partial(leave_kernel, part),
+        call_id,
+        "leave",
+        (product, residual),
+        [jax.ShapeDtypeStruct((rows, n_dp * part), bf16)],
+        [pltpu.VMEM((n_dp, rows, part), f32), pltpu.VMEM((n_dp, rows, part), bf16)]
+        + add_up_scratch("ctx", [(n_dp, rows, part)])
+        + dma_sems(n_dp)
+        + [pltpu.SemaphoreType.DMA],
+    )[0]
+
+
+def attend_kernel(group, sets, rows, chunk, first_free, at_ref, q_ref, k_ref, v_ref, m_ref, o_ref, acc, total):
     step = pl.program_id(0)
+    wide_head = group * HD
 
     @pl.when(step == 0)
     def _():
         acc[...] = jnp.zeros_like(acc)
         total[...] = jnp.zeros_like(total)
 
-    ones = jnp.ones((8, HD), bf16)
     over_width = (((1,), (1,)), ((), ()))
+    of_head = lax.broadcasted_iota(jnp.int32, (8 * group, wide_head), 0) // 8
+    in_head = lax.broadcasted_iota(jnp.int32, (8 * group, wide_head), 1) // HD
+    ones = jnp.where(of_head == in_head, 1.0, 0.0).astype(bf16)
 
     def add_chunk(masked):
         is_first = m_ref[...] == 0
-        for head in range(heads):
-            cut = slice(head * HD, (head + 1) * HD)
+        for one in range(sets):
+            cut = slice(one * wide_head, (one + 1) * wide_head)
             keys = k_ref[:, cut]
-            both = lax.dot_general(q_ref[head], keys, over_width, preferred_element_type=f32)
+            both = lax.dot_general(q_ref[one], keys, over_width, preferred_element_type=f32)
             wide = keys.astype(f32)
             squares = lax.dot_general(
                 ones, (wide * wide).astype(bf16), over_width, preferred_element_type=f32
-            )[:1]
+            )
             inverse = lax.rsqrt(squares * (1.0 / HD) + epsilon)
-            probs = jnp.exp(jnp.where(is_first, both[:rows], both[rows:]) * inverse)
-            if masked:
-                key_pos = step * chunk + lax.broadcasted_iota(jnp.int32, (rows, chunk), 1)
-                row_pos = lax.broadcasted_iota(jnp.int32, (rows, chunk), 0)
-                probs = jnp.where(key_pos <= first_free + at_ref[1] + row_pos, probs, 0.0)
-            total[head] += jnp.sum(probs, axis=1, keepdims=True)
-            acc[head] += jnp.dot(probs.astype(bf16), v_ref[:, cut], preferred_element_type=f32)
+            parts = []
+            for h in range(group):
+                at = 2 * h * rows
+                scores = jnp.where(is_first, both[at : at + rows], both[at + rows : at + 2 * rows])
+                probs = jnp.exp(scores * inverse[8 * h : 8 * h + 1])
+                if masked:
+                    key_pos = step * chunk + lax.broadcasted_iota(jnp.int32, (rows, chunk), 1)
+                    row_pos = lax.broadcasted_iota(jnp.int32, (rows, chunk), 0)
+                    probs = jnp.where(key_pos <= first_free + at_ref[1] + row_pos, probs, 0.0)
+                total[one * group + h] += jnp.sum(probs, axis=1, keepdims=True)
+                parts.append(probs.astype(bf16))
+            acc[one] += jnp.dot(
+                jnp.concatenate(parts, axis=0), v_ref[:, cut], preferred_element_type=f32
+            )
 
     has_free = (step + 1) * chunk > first_free
 
@@ -274,8 +341,10 @@
 
     @pl.when(step == pl.num_programs(0) - 1)
     def _():
-        for head in range(heads):
-            o_ref[:, head * HD : (head + 1) * HD] = (acc[head] / total[head]).astype(bf16)
+        for head in range(sets * group):
+            one, h = head // group, head % group
+            summed = acc[one, h * rows : (h + 1) * rows, h * HD : (h + 1) * HD]
+            o_ref[:, head * HD : (head + 1) * HD] = (summed / total[head]).astype(bf16)
 
 
 def attend(queries, key_cache, value_cache, key_modality, column, row_start, slab_len):
@@ -284,22 +353,27 @@
     cache_len = key_cache.shape[0]
     chunk = min(1024, cache_len)
     width = heads * HD
+    group = 2 if heads % 2 == 0 else 1
+    sets = heads // group
+    apart = jnp.eye(group, dtype=bf16)[None, :, None, :, None]
+    queries = queries.reshape(sets, group, double, 1, HD) * apart
+    queries = queries.reshape(sets, group * double, group * HD)
     where_at = jnp.stack([column, row_start]).astype(jnp.int32)
     return pl.pallas_call(
-        functools.partial(attend_kernel, heads, rows, chunk, cache_len - slab_len),
+        functools.partial(attend_kernel, group, sets, rows, chunk, cache_len - slab_len),
         out_shape=jax.ShapeDtypeStruct((rows, width), bf16),
         grid_spec=pltpu.PrefetchScalarGridSpec(
             num_scalar_prefetch=1,
             grid=(cache_len // chunk,),
             in_specs=[
-                pl.BlockSpec((heads, double, HD), lambda j, at: (0, 0, 0)),
+                pl.BlockSpec((sets, group * double, group * HD), lambda j, at: (0, 0, 0)),
                 pl.BlockSpec((chunk, width), lambda j, at: (j, at[0])),
                 pl.BlockSpec((chunk, width), lambda j, at: (j, at[0])),
                 pl.BlockSpec((1, chunk), lambda j, at: (0, j)),
             ],
             out_specs=pl.BlockSpec((rows, width), lambda j, at: (0, 0)),
             scratch_shapes=[
-                pltpu.VMEM((heads, rows, HD), f32),
+                pltpu.VMEM((sets, group * rows, group * HD), f32),
                 pltpu.VMEM((heads, rows, 1), f32),
             ],
         ),
@@ -434,26 +508,14 @@
             head_out, "dp", (n_dp, n_mod, count, width), lambda ref, j, i: ref.at[i, j], 2
         )
 
-    def to_blocks(values, weight, call_id):
+    def own_product(values, weight):
         values = values.reshape(tokens, values.shape[-1])
         masked = jnp.where(is_mine.reshape(tokens, 1), values, jnp.zeros_like(values))
         product = jnp.dot(masked, weight, preferred_element_type=f32).astype(bf16)
-        product = product.reshape(n_dp, n_mod, n_ctx, rows, part)
-        return reduce(
-            (product,), "ctx", lambda ref, j, i: ref.at[:, j, i], [(n_dp, rows, part)], call_id
-        )[0]
-
-    attention = to_blocks(shared, out_weight[0], 3)
-    residual = own_block[..., :part].astype(f32) + attention
-    squares = jnp.sum(residual * residual, axis=-1)
-
-    slab = gather(
-        beside(residual, two_parts(squares)),
-        "ctx",
-        (n_dp, n_mod, n_ctx, rows, part + LANES),
-        lambda ref, j, i: ref.at[:, j, i],
-        4,
-    )
+        return product.reshape(n_dp, n_mod, n_ctx, rows, part)
+
+    residual, slab = renew(own_product(shared, out_weight[0]), own_block, 3)
+
     gain = lax.dynamic_slice_in_dim(norm_ffn[0], d * part, part)
     scaled = jnp.where(is_mine[..., None], slab[..., :part].astype(f32) * gain, 0.0)
     scaled = scaled.astype(bf16).reshape(tokens, part)
@@ -477,9 +539,7 @@
     shared = gather(
         activated, "dp", (*by_block, hidden_units), lambda ref, j, i: ref.at[i, j], 6
     )
-    mixed = residual + to_blocks(shared, down_weight[0], 7)
-    home = to_home(mixed.astype(bf16), 8)
-    return home.transpose(1, 0, 2).reshape(1, rows, model)
+    return leave(own_product(shared, down_weight[0]), residual, 7)[None]
 
 
 def solution(mesh):

time: 185 us -> 176 us (0.951)
  Pallas kernels: 134 us -> 127 us
  other arithmetic: 21.6 us -> 18.4 us
    pallas_call x9 -> x7, Pallas kernels: 119 us -> 113 us  [communicate(): pl.pallas_call(kernel, out_shape=outs, in_specs=[whole] * len(operands),...]
    convert_element_type x2 -> x1, other arithmetic: 2.57 us -> 0.01 us  [attend(): apart = jnp.eye(group, dtype=bf16)[None, :, None, :, None]]
where the time goes in v3:
time: 176 us; the launch traced here: 175 us
  Pallas kernels  127 us (72%)
  other arithmetic  18.4 us (10%)
  matrix products  17.6 us (10%)
  local copies, waits for them, and re-layouts  11.3 us (6%)
    pallas_call x7, Pallas kernels, communicate(): pl.pallas_call(kernel, out_shape=outs, in_specs=[whole] * len(operands),...  113 us
    pallas_call x1, Pallas kernels, attend(): pl.pallas_call(functools.partial(attend_kernel, group, sets, rows, chunk,...  13.9 us
    dot_general x2, matrix products, own_product(): product = jnp.dot(masked, weight, preferred_element_type=f32).astype(bf16)  8.38 us
    dot_general x1, matrix products, per_device(): up = jnp.dot(scaled, up_weight[0], preferred_element_type=f32).astype(bf16)  4.27 us
    dot_general x1, matrix products, per_device(): jnp.dot(scaled, gate_weight[0], preferred_element_type=f32).astype(bf16)  4.26 us

profile of v3, /device:TPU:0, one launch (start us, length us, event | category | flops | bytes accessed | tf_op | source)
XLA Modules:
  0.0 174.9 jit_solution(1412842074323371474)
XLA Ops:
  0.0 1.1 multiply_reduce_fusion.1
  1.2 0.7 convert_bitcast_fusion
  1.8 0.6 pad_add_fusion.at_ref
  2.6 0.1 copy.47
  2.7 0.7 dynamic-slice_bitcast_fusion
  3.4 0.7 constant_dynamic-slice_fusion
  4.1 0.8 fusion.30
  5.0 1.5 pad_maximum_fusion.x_ref
  6.5 0.1 mul.170
  6.7 17.7 %enter.1 = (bf16[4,8,1152]{2,1,0:T(8,128)(2,1)}, bf16[4,2,4,8,1152]{4,3,2,1,0:T(8,128)(2,1)}) custom-call(bf16[4,8,1152]{2,1,0:T(8,128)(2,1)} %pad_maximum_fusion.x_ref), custom_call_target="tpu_custom_call" | custom-call | tf_op jit(solution)/shard_map/enter/pallas_call | solution.py:97
  24.4 0.9 slice_convert_fusion
  25.2 0.6 compare_reduce_fusion
  25.9 0.7 eq.56
  26.6 0.2 fusion.28
  26.9 1.3 select_convert_fusion.1
  28.2 0.2 fusion.26
  28.4 0.6 eq.62
  29.0 0.7 fusion.16
  29.8 0.4 concatenate.10
  30.2 0.9 maximum_bitcast_fusion.refs_0_
  31.1 10.2 %reduce_1_dp.1 = f32[80,512]{1,0:T(8,128)} custom-call(bf16[4,2,80,512]{3,2,1,0:T(8,128)(2,1)} %maximum_bitcast_fusion.refs_0_), custom_call_target="tpu_custom_call" | custom-call | tf_op jit(solution)/shard_map/reduce_1_dp/pallas_call | solution.py:97
  41.4 0.7 slice.49
  42.1 0.7 slice.48
  42.8 0.9 slice.47
  43.8 0.1 multiply_reduce_fusion
  44.0 0.2 multiply_bitcast_fusion
  44.3 0.1 mul.168
  44.4 0.2 mul.169
  44.6 0.7 broadcast_multiply_fusion.q_ref
  45.3 13.9 %attend.1.x_ref = bf16[64,512]{1,0:T(8,128)(2,1)} custom-call(s32[2]{0:T(128)} %pad_add_fusion.at_ref, bf16[2,256,256]{2,1,0:T(8,128)(2,1)} %broadcast_multiply_fusion.q_ref, bf16[8192,1024]{1,0:T(8,128)(2,1)} %bitcast.78, bf16[8192,1024]{1,0:T(8,128)(2,1)} %bitcast.79, s32[1,8192]{1,0:T(1,128)} %m_ref.1), custom_call_target="tpu_custom_call" | custom-call | tf_op jit(solution)/shard_map/attend/pallas_call | solution.py:362
  59.2 9.1 %gather_2_dp.1 = bf16[4,64,1024]{2,1,0:T(8,128)(2,1)} custom-call(bf16[64,512]{1,0:T(8,128)(2,1)} %attend.1.x_ref), custom_call_target="tpu_custom_call" | custom-call | tf_op jit(solution)/shard_map/gather_2_dp/pallas_call | solution.py:97
  68.3 1.1 broadcast_select_fusion.1
  69.4 3.1 %fusion.19 = bf16[256,1024]{1,0:T(8,128)(2,1)} fusion(bf16[256,1024]{1,0:T(8,128)(2,1)S(1)} %bitcast.91, bf16[1,1024,1024]{2,1,0:T(8,128)(2,1)} %param.23), kind=kOutput, calls=%fused_computation.14 | convolution fusion | flops 537133056 | bytes 3145728 | tf_op jit(solution)/shard_map/dot_general | solution.py:514
  72.5 20.6 %renew.1 = (f32[4,8,1024]{2,1,0:T(8,128)}, bf16[4,2,4,8,1152]{4,3,2,1,0:T(8,128)(2,1)}) custom-call(bf16[4,2,4,8,1024]{4,3,2,1,0:T(8,128)(2,1)} %bitcast.85, bf16[4,8,1152]{2,1,0:T(8,128)(2,1)} %get-tuple-element.13.own_ref), custom_call_target="tpu_custom_call" | custom-call | tf_op jit(solution)/shard_map/renew/pallas_call | solution.py:97
  93.1 1.6 select_bitcast_fusion.refs_2_
  94.7 1.2 select_convert_fusion
  95.9 4.3 %fusion.9 = bf16[256,2752]{0,1:T(8,128)(2,1)S(1)} fusion(bf16[256,1024]{1,0:T(8,128)(2,1)S(1)} %bitcast.87, bf16[1,1024,2752]{1,2,0:T(8,128)(2,1)} %param.26), kind=kOutput, calls=%fused_computation.7 | convolution fusion | flops 1443545088 | bytes 7569408 | tf_op jit(solution)/shard_map/dot_general | solution.py:524
  100.2 1.7 copy.45
  101.9 4.3 %fusion.6 = bf16[256,2752]{0,1:T(8,128)(2,1)S(1)} fusion(bf16[256,1024]{1,0:T(8,128)(2,1)S(1)} %bitcast.88, bf16[1,1024,2752]{1,2,0:T(8,128)(2,1)} %param.25), kind=kOutput, calls=%fused_computation.6 | convolution fusion | flops 1443545088 | bytes 7569408 | tf_op jit(solution)/shard_map/dot_general | solution.py:523
  106.1 1.7 copy.44
  107.8 24.5 %reduce_5_dp.1 = (f32[32,2752]{1,0:T(8,128)}, f32[32,2752]{1,0:T(8,128)}, f32[32,128]{1,0:T(8,128)}) custom-call(bf16[4,2,32,2752]{3,2,1,0:T(8,128)(2,1)} %bitcast.81, bf16[4,2,32,2752]{3,2,1,0:T(8,128)(2,1)} %bitcast.80, bf16[4,2,32,128]{3,2,1,0:T(8,128)(2,1)} %select_bitcast_fusion.refs_2_), custom_call_target="tpu_custom_call" | custom-call | tf_op jit(solution)/shard_map/reduce_5_dp/pallas_call | solution.py:97
  132.3 1.0 rsqrt_reduce_fusion
  133.3 1.9 %multiply_convert_fusion.x_ref = bf16[32,2752]{1,0:T(8,128)(2,1)} fusion(f32[32,2752]{1,0:T(8,128)} %get-tuple-element.17, f32[32,2752]{1,0:T(8,128)} %get-tuple-element.15, f32[32]{0:T(128)S(1)} %rsqrt_reduce_fusion), kind=kLoop, calls=%fused_computation.20 | loop fusion | flops 704512 | bytes 880768 | tf_op jit(solution)/shard_map/convert_element_type | solution.py:538
  135.2 14.5 %gather_6_dp.1 = bf16[4,2,32,2752]{3,2,1,0:T(8,128)(2,1)} custom-call(bf16[32,2752]{1,0:T(8,128)(2,1)} %multiply_convert_fusion.x_ref), custom_call_target="tpu_custom_call" | custom-call | tf_op jit(solution)/shard_map/gather_6_dp/pallas_call | solution.py:97
  149.7 1.5 broadcast_select_fusion
  151.3 5.3 %fusion.22 = bf16[256,1024]{1,0:T(8,128)(2,1)} fusion(bf16[256,2752]{1,0:T(8,128)(2,1)S(1)} %bitcast.82, bf16[1,2752,1024]{2,1,0:T(8,128)(2,1)} %param.27), kind=kOutput, calls=%fused_computation.15 | convolution fusion | flops 1443102720 | bytes 7569408 | tf_op jit(solution)/shard_map/dot_general | solution.py:514
  156.6 16.8 %leave.1 = bf16[8,4096]{1,0:T(8,128)(2,1)} custom-call(bf16[4,2,4,8,1024]{4,3,2,1,0:T(8,128)(2,1)} %bitcast.89, f32[4,8,1024]{2,1,0:T(8,128)} %get-tuple-element.18.residual_ref), custom_call_target="tpu_custom_call" | custom-call | tf_op jit(solution)/shard_map/leave/pallas_call | solution.py:97
  173.4 1.5 copy.56
  (33 shorter events, 0.6 us)
Async XLA Ops:
  0.0 29.0 %copy-start = (bf16[1,1024,1024]{2,1,0:T(8,128)(2,1)S(1)}, bf16[1,1024,1024]{2,1,0:T(8,128)(2,1)}, u32[]{:S(2)}) copy-start(bf16[1,1024,1024]{2,1,0:T(8,128)(2,1)} %param.20) | copy-start | bytes 6291460
  30.2 13.8 %copy-start.3 = (pred[64]{0:T(512)(128)(4,1)S(1)}, pred[64]{0:T(512)(128)(4,1)}, u32[]{:S(2)}) copy-start(pred[64]{0:T(512)(128)(4,1)} %eq.62) | copy-start | bytes 196
  45.3 23.0 %copy-start.2 = (pred[4,64]{1,0:T(4,128)(4,1)S(1)}, pred[4,64]{1,0:T(4,128)(4,1)}, u32[]{:S(2)}) copy-start(pred[4,64]{1,0:T(4,128)(4,1)} %eq.56) | copy-start | bytes 772
  151.3 23.6 %copy-start.1 = (bf16[1,1024,1024]{2,1,0:T(8,128)(2,1)S(1)}, bf16[1,1024,1024]{2,1,0:T(8,128)(2,1)}, u32[]{:S(2)}) copy-start(bf16[1,1024,1024]{2,1,0:T(8,128)(2,1)} %param.20) | copy-start | bytes 6291460

commit v4 on v3

--- a/solution.py
+++ b/solution.py
@@ -260,6 +260,65 @@
         + dma_sems(n_ctx, n_mod * n_ctx)
         + [pltpu.SemaphoreType.DMA],
     )
+
+
+def block_of_dp(ref, j, i):
+    return ref.at[i, j]
+
+
+def activate_kernel(model, gate_ref, up_ref, tag_ref, o_ref, gate_sum, up_sum, tag_sum, message, *refs):
+    s1, r1, s2, r2, own_sem = refs[-5:]
+    greet(("dp", "mod"))
+    sums = (gate_sum, up_sum, tag_sum)
+    add_up("dp", 3, block_of_dp, (gate_ref, up_ref, tag_ref), sums, *refs[:-5])
+    squares = tag_sum[:, :1] + tag_sum[:, 1:2]
+    inverse = lax.rsqrt(squares * (1.0 / model) + epsilon)
+    gate = gate_sum[...] * inverse
+    message[...] = (gate / (1.0 + jnp.exp(-gate)) * (up_sum[...] * inverse)).astype(bf16)
+    spread("dp", message, lambda j, i: block_of_dp(o_ref, j, i), (s1, r1), (s2, r2), own_sem)
+
+
+def activate(gate, up, tags, model, call_id):
+    n_dp, n_mod, count, hidden_units = gate.shape
+    shapes = [(count, hidden_units)] * 2 + [(count, LANES)]
+    return communicate(
+        functools.partial(activate_kernel, model),
+        call_id,
+        "activate",
+        (gate, up, tags),
+        [jax.ShapeDtypeStruct(gate.shape, bf16)],
+        [pltpu.VMEM(shape, f32) for shape in shapes]
+        + [pltpu.VMEM((count, hidden_units), bf16)]
+        + add_up_scratch("dp", shapes)
+        + dma_sems(n_dp, n_mod * n_dp)
+        + [pltpu.SemaphoreType.DMA],
+    )[0]
+
+
+def expand_kernel(x_ref, gate_ref, up_ref, gate_out, up_out):
+    x = x_ref[...]
+    gate_out[...] = jnp.dot(x, gate_ref[...], preferred_element_type=f32).astype(bf16)
+    up_out[...] = jnp.dot(x, up_ref[...], preferred_element_type=f32).astype(bf16)
+
+
+def expand(x, gate_weight, up_weight):
+    tokens, part = x.shape
+    hidden_units = gate_weight.shape[1]
+    tile = min(512, hidden_units)
+    weight = pl.BlockSpec((part, tile), lambda j: (0, j))
+    product = pl.BlockSpec((tokens, tile), lambda j: (0, j))
+    out = jax.ShapeDtypeStruct((tokens, hidden_units), bf16)
+    return pl.pallas_call(
+        expand_kernel,
+        grid=(pl.cdiv(hidden_units, tile),),
+        in_specs=[pl.BlockSpec((tokens, part), lambda j: (0, 0)), weight, weight],
+        out_specs=[product, product],
+        out_shape=[out, out],
+        compiler_params=pltpu.CompilerParams(
+            dimension_semantics=("arbitrary",), vmem_limit_bytes=60 * 2**20
+        ),
+        name="expand",
+    )(x, gate_weight, up_weight)
 
 
 def leave_kernel(part, x_ref, residual_ref, o_ref, total, message, *refs):
@@ -510,8 +569,8 @@
 
     def own_product(values, weight):
         values = values.reshape(tokens, values.shape[-1])
-        masked = jnp.where(is_mine.reshape(tokens, 1), values, jnp.zeros_like(values))
-        product = jnp.dot(masked, weight, preferred_element_type=f32).astype(bf16)
+        product = jnp.dot(values, weight, preferred_element_type=f32)
+        product = jnp.where(is_mine.reshape(tokens, 1), product, 0.0).astype(bf16)
         return product.reshape(n_dp, n_mod, n_ctx, rows, part)
 
     residual, slab = renew(own_product(shared, out_weight[0]), own_block, 3)
@@ -520,24 +579,14 @@
     scaled = jnp.where(is_mine[..., None], slab[..., :part].astype(f32) * gain, 0.0)
     scaled = scaled.astype(bf16).reshape(tokens, part)
     by_block = (n_dp, n_mod, n_ctx * rows)
-    gate = jnp.dot(scaled, gate_weight[0], preferred_element_type=f32).astype(bf16)
-    up = jnp.dot(scaled, up_weight[0], preferred_element_type=f32).astype(bf16)
+    gate, up = expand(scaled, gate_weight[0], up_weight[0])
     squares = jnp.where(is_mine[..., None], slab[..., part:], jnp.zeros_like(slab[..., part:]))
-    gate, up, squares = reduce(
-        (
-            gate.reshape(*by_block, hidden_units),
-            up.reshape(*by_block, hidden_units),
-            squares.reshape(*by_block, LANES),
-        ),
-        "dp",
-        lambda ref, j, i: ref.at[i, j],
-        [(n_ctx * rows, hidden_units)] * 2 + [(n_ctx * rows, LANES)],
+    shared = activate(
+        gate.reshape(*by_block, hidden_units),
+        up.reshape(*by_block, hidden_units),
+        squares.reshape(*by_block, LANES),
+        model,
         5,
-    )
-    inverse = lax.rsqrt((squares[:, :1] + squares[:, 1:2]) * (1.0 / model) + epsilon)
-    activated = (jax.nn.silu(gate * inverse) * (up * inverse)).astype(bf16)
-    shared = gather(
-        activated, "dp", (*by_block, hidden_units), lambda ref, j, i: ref.at[i, j], 6
     )
     return leave(own_product(shared, down_weight[0]), residual, 7)[None]
 

time: 176 us -> 182 us (1.034)
  local copies, waits for them, and re-layouts: 11.3 us -> 24 us
  matrix products: 17.6 us -> 8.89 us
  Pallas kernels: 127 us -> 134 us
  other arithmetic: 18.4 us -> 13.6 us
    unnamed x11 -> x13, local copies, waits for them, and re-layouts: 1.61 us -> 18.4 us
    pallas_call x0 -> x1, Pallas kernels: none -> 9.2 us  [expand(): pl.pallas_call(expand_kernel, grid=(pl.cdiv(hidden_units, tile),), in_spe...]
    dot_general x4 -> x2, matrix products: 16.9 us -> 8.18 us  [own_product(): product = jnp.dot(values, weight, preferred_element_type=f32)]
    convert_element_type x2 -> x0, local copies, waits for them, and re-layouts: 3.4 us -> none  [the longest x1 1.71 us: per_device(): up = jnp.dot(scaled, up_weight[0], preferred_element_type=f32).astype(bf16)]
    select_n x2 -> x0, other arithmetic: 2.67 us -> none  [own_product(): jnp.where(is_mine.reshape(tokens, 1), values, jnp.zeros_like(values))]
    pallas_call x7 -> x6, Pallas kernels: 113 us -> 111 us  [communicate(): pl.pallas_call(kernel, out_shape=outs, in_specs=[whole] * len(operands),...]
    convert_element_type x1 -> x0, other arithmetic: 1.95 us -> none  [per_device(): activated = (jax.nn.silu(gate * inverse) * (up * inverse)).astype(bf16)]
where the time goes in v4:
time: 182 us; the launch traced here: 181 us
  Pallas kernels  134 us (74%)
  local copies, waits for them, and re-layouts  24 us (13%)
  other arithmetic  13.6 us (7%)
  matrix products  8.89 us (5%)
    pallas_call x6, Pallas kernels, communicate(): pl.pallas_call(kernel, out_shape=outs, in_specs=[whole] * len(operands),...  111 us
    unnamed x13, local copies, waits for them, and re-layouts  18.4 us
    pallas_call x1, Pallas kernels, attend(): pl.pallas_call(functools.partial(attend_kernel, group, sets, rows, chunk,...  13.9 us
    pallas_call x1, Pallas kernels, expand(): pl.pallas_call(expand_kernel, grid=(pl.cdiv(hidden_units, tile),), in_spe...  9.2 us
    dot_general x2, matrix products, own_product(): product = jnp.dot(values, weight, preferred_element_type=f32)  8.18 us

profile of v4, /device:TPU:0, one launch (start us, length us, event | category | flops | bytes accessed | tf_op | source)
XLA Modules:
  0.0 180.9 jit_solution(3595223408795387879)
XLA Ops:
  0.0 1.1 multiply_reduce_fusion.1
  1.2 0.7 convert_bitcast_fusion
  1.8 0.6 pad_add_fusion.at_ref
  2.5 0.1 broadcast_in_dim.139
  2.5 0.1 broadcast_in_dim.140
  2.6 0.1 copy.40
  2.7 0.7 dynamic-slice_bitcast_fusion
  3.4 0.7 constant_dynamic-slice_fusion
  4.1 0.8 fusion.26
  4.9 0.1 broadcast_select_fusion
  5.0 1.5 pad_maximum_fusion.x_ref
  6.5 0.1 mul.141
  6.7 17.7 %enter.1 = (bf16[4,8,1152]{2,1,0:T(8,128)(2,1)}, bf16[4,2,4,8,1152]{4,3,2,1,0:T(8,128)(2,1)}) custom-call(bf16[4,8,1152]{2,1,0:T(8,128)(2,1)} %pad_maximum_fusion.x_ref), custom_call_target="tpu_custom_call" | custom-call | tf_op jit(solution)/shard_map/enter/pallas_call | solution.py:97
  24.4 0.9 slice_convert_fusion
  25.2 0.6 compare_reduce_fusion
  25.9 0.7 eq.51
  26.5 0.2 fusion.24
  26.8 1.3 select_convert_fusion.1
  28.1 0.2 fusion.22
  28.4 0.1 eq.57
  28.4 0.0 copy-done
  28.5 0.7 fusion.15
  29.2 0.4 concatenate.10
  29.6 0.1 copy.34
  29.6 0.9 maximum_bitcast_fusion.refs_0_
  30.5 10.2 %reduce_1_dp.1 = f32[80,512]{1,0:T(8,128)} custom-call(bf16[4,2,80,512]{3,2,1,0:T(8,128)(2,1)} %maximum_bitcast_fusion.refs_0_), custom_call_target="tpu_custom_call" | custom-call | tf_op jit(solution)/shard_map/reduce_1_dp/pallas_call | solution.py:97
  40.8 0.7 slice.43
  41.5 0.7 slice.42
  42.2 0.9 slice.41
  43.2 0.1 multiply_reduce_fusion
  43.4 0.2 multiply_bitcast_fusion
  43.6 0.1 mul.139
  43.8 0.2 mul.140
  44.0 0.7 broadcast_multiply_fusion.q_ref
  44.7 13.9 %attend.1.x_ref = bf16[64,512]{1,0:T(8,128)(2,1)} custom-call(s32[2]{0:T(128)} %pad_add_fusion.at_ref, bf16[2,256,256]{2,1,0:T(8,128)(2,1)} %broadcast_multiply_fusion.q_ref, bf16[8192,1024]{1,0:T(8,128)(2,1)} %bitcast.74, bf16[8192,1024]{1,0:T(8,128)(2,1)} %bitcast.75, s32[1,8192]{1,0:T(1,128)} %m_ref.1), custom_call_target="tpu_custom_call" | custom-call | tf_op jit(solution)/shard_map/attend/pallas_call | solution.py:421
  58.6 9.1 %gather_2_dp.1 = bf16[4,64,1024]{2,1,0:T(8,128)(2,1)} custom-call(bf16[64,512]{1,0:T(8,128)(2,1)} %attend.1.x_ref), custom_call_target="tpu_custom_call" | custom-call | tf_op jit(solution)/shard_map/gather_2_dp/pallas_call | solution.py:97
  67.7 2.5 %fusion.18 = bf16[256,1024]{1,0:T(8,128)(2,1)} fusion(bf16[256,1024]{1,0:T(8,128)(2,1)} %bitcast.83, bf16[1,1024,1024]{2,1,0:T(8,128)(2,1)S(1)} %copy-done.3, pred[256]{0:T(512)(128)(4,1)S(1)} %copy-done.2), kind=kOutput, calls=%fused_computation.10 | convolution fusion | flops 537395200 | bytes 3145984 | tf_op jit(solution)/shard_map/dot_general | solution.py:572
  70.2 20.7 %renew.1 = (f32[4,8,1024]{2,1,0:T(8,128)}, bf16[4,2,4,8,1152]{4,3,2,1,0:T(8,128)(2,1)}) custom-call(bf16[4,2,4,8,1024]{4,3,2,1,0:T(8,128)(2,1)} %bitcast.82, bf16[4,8,1152]{2,1,0:T(8,128)(2,1)} %get-tuple-element.12.own_ref), custom_call_target="tpu_custom_call" | custom-call | tf_op jit(solution)/shard_map/renew/pallas_call | solution.py:97
  90.9 1.6 select_bitcast_fusion.tag_ref
  92.4 2.0 %select_convert_fusion = bf16[4,2,4,8,1024]{4,3,2,1,0:T(8,128)(2,1)} fusion(f32[1024]{0:T(1024)S(1)} %bitcast.91, bf16[4,2,4,8,1152]{4,3,2,1,0:T(8,128)(2,1)} %get-tuple-element.13, pred[4,2,4,8]{3,2,1,0:T(4,128)(4,1)S(1)} %compare_reduce_fusion), kind=kLoop, calls=%fused_computation.11 | loop fusion | flops 1048576 | bytes 1052928 | tf_op jit(solution)/shard_map/convert_element_type | solution.py:580
  94.4 8.3 %copy.38 = bf16[1,1024,2752]{2,1,0:T(8,128)(2,1)} copy(bf16[1,1024,2752]{1,2,0:T(8,128)(2,1)} %param.25) | data formatting | bytes 11272192 | tf_op args[11]
  102.8 8.4 %copy.39 = bf16[1,1024,2752]{2,1,0:T(8,128)(2,1)} copy(bf16[1,1024,2752]{1,2,0:T(8,128)(2,1)} %param.26) | data formatting | bytes 11272192 | tf_op args[12]
  111.2 9.2 %expand.1 = (bf16[256,2752]{1,0:T(8,128)(2,1)}, bf16[256,2752]{1,0:T(8,128)(2,1)}) custom-call(bf16[256,1024]{1,0:T(8,128)(2,1)} %bitcast.76, bf16[1024,2752]{1,0:T(8,128)(2,1)} %bitcast.72, bf16[1024,2752]{1,0:T(8,128)(2,1)} %bitcast.73), custom_call_target="tpu_custom_call" | custom-call | tf_op jit(solution)/shard_map/expand/pallas_call | solution.py:311
  120.4 36.0 %activate.1 = bf16[4,2,32,2752]{3,2,1,0:T(8,128)(2,1)} custom-call(bf16[4,2,32,2752]{3,2,1,0:T(8,128)(2,1)} %bitcast.77, bf16[4,2,32,2752]{3,2,1,0:T(8,128)(2,1)} %bitcast.78, bf16[4,2,32,128]{3,2,1,0:T(8,128)(2,1)} %select_bitcast_fusion.tag_ref), custom_call_target="tpu_custom_call" | custom-call | tf_op jit(solution)/shard_map/activate/pallas_call | solution.py:97
  156.4 0.0 copy-start.1
  156.4 5.6 %fusion.12 = bf16[256,1024]{1,0:T(8,128)(2,1)} fusion(bf16[256,2752]{1,0:T(8,128)(2,1)} %bitcast.79, bf16[1,2752,1024]{2,1,0:T(8,128)(2,1)} %param.27, pred[256]{0:T(512)(128)(4,1)S(1)} %copy-done.2), kind=kOutput, calls=%fused_computation.8 | convolution fusion | flops 1443364864 | bytes 7569664 | tf_op jit(solution)/shard_map/dot_general | solution.py:572
  162.0 17.4 %leave.1 = bf16[8,4096]{1,0:T(8,128)(2,1)} custom-call(bf16[4,2,4,8,1024]{4,3,2,1,0:T(8,128)(2,1)} %bitcast.85, f32[4,8,1024]{2,1,0:T(8,128)} %get-tuple-element.16.residual_ref), custom_call_target="tpu_custom_call" | custom-call | tf_op jit(solution)/shard_map/leave/pallas_call | solution.py:97
  179.4 1.5 copy.49
  (26 shorter events, 0.3 us)
Async XLA Ops:
  0.0 28.4 %copy-start = (bf16[1,1024,1024]{2,1,0:T(8,128)(2,1)S(1)}, bf16[1,1024,1024]{2,1,0:T(8,128)(2,1)}, u32[]{:S(2)}) copy-start(bf16[1,1024,1024]{2,1,0:T(8,128)(2,1)} %param.20) | copy-start | bytes 6291460
  44.7 23.0 %copy-start.2 = (pred[256]{0:T(512)(128)(4,1)S(1)}, pred[256]{0:T(512)(128)(4,1)}, u32[]{:S(2)}) copy-start(pred[256]{0:T(512)(128)(4,1)} %eq.51) | copy-start | bytes 772
  44.7 23.0 %copy-start.3 = (bf16[1,1024,1024]{2,1,0:T(8,128)(2,1)S(1)}, bf16[1,1024,1024]{2,1,0:T(8,128)(2,1)}, u32[]{:S(2)}) copy-start(bf16[1,1024,1024]{2,1,0:T(8,128)(2,1)} %param.23) | copy-start | bytes 6291460
  156.4 24.5 %copy-start.1 = (bf16[1,1024,1024]{2,1,0:T(8,128)(2,1)S(1)}, bf16[1,1024,1024]{2,1,0:T(8,128)(2,1)}, u32[]{:S(2)}) copy-start(bf16[1,1024,1024]{2,1,0:T(8,128)(2,1)} %param.20) | copy-start | bytes 6291460

commit v5 on v4

--- a/solution.py
+++ b/solution.py
@@ -297,15 +297,17 @@
 
 def expand_kernel(x_ref, gate_ref, up_ref, gate_out, up_out):
     x = x_ref[...]
-    gate_out[...] = jnp.dot(x, gate_ref[...], preferred_element_type=f32).astype(bf16)
-    up_out[...] = jnp.dot(x, up_ref[...], preferred_element_type=f32).astype(bf16)
+    over_width = (((1,), (1,)), ((), ()))
+    for weight, out in ((gate_ref, gate_out), (up_ref, up_out)):
+        product = lax.dot_general(x, weight[...], over_width, preferred_element_type=f32)
+        out[...] = product.astype(bf16)
 
 
 def expand(x, gate_weight, up_weight):
     tokens, part = x.shape
-    hidden_units = gate_weight.shape[1]
+    hidden_units = gate_weight.shape[0]
     tile = min(512, hidden_units)
-    weight = pl.BlockSpec((part, tile), lambda j: (0, j))
+    weight = pl.BlockSpec((tile, part), lambda j: (j, 0))
     product = pl.BlockSpec((tokens, tile), lambda j: (0, j))
     out = jax.ShapeDtypeStruct((tokens, hidden_units), bf16)
     return pl.pallas_call(
@@ -579,7 +581,7 @@
     scaled = jnp.where(is_mine[..., None], slab[..., :part].astype(f32) * gain, 0.0)
     scaled = scaled.astype(bf16).reshape(tokens, part)
     by_block = (n_dp, n_mod, n_ctx * rows)
-    gate, up = expand(scaled, gate_weight[0], up_weight[0])
+    gate, up = expand(scaled, gate_weight[0].T, up_weight[0].T)
     squares = jnp.where(is_mine[..., None], slab[..., part:], jnp.zeros_like(slab[..., part:]))
     shared = activate(
         gate.reshape(*by_block, hidden_units),

time: 182 us -> 165 us (0.907)
  local copies, waits for them, and re-layouts: 24 us -> 7.3 us
    unnamed x13 -> x11, local copies, waits for them, and re-layouts: 18.4 us -> 1.61 us
where the time goes in v5:
time: 165 us; the launch traced here: 164 us
  Pallas kernels  134 us (81%)
  other arithmetic  13.7 us (8%)
  matrix products  8.88 us (5%)
  local copies, waits for them, and re-layouts  7.3 us (4%)
    pallas_call x6, Pallas kernels, communicate(): pl.pallas_call(kernel, out_shape=outs, in_specs=[whole] * len(operands),...  111 us
    pallas_call x1, Pallas kernels, attend(): pl.pallas_call(functools.partial(attend_kernel, group, sets, rows, chunk,...  13.9 us
    pallas_call x1, Pallas kernels, expand(): pl.pallas_call(expand_kernel, grid=(pl.cdiv(hidden_units, tile),), in_spe...  9 us
    dot_general x2, matrix products, own_product(): product = jnp.dot(values, weight, preferred_element_type=f32)  8.17 us

profile of v5, /device:TPU:0, one launch (start us, length us, event | category | flops | bytes accessed | tf_op | source)
XLA Modules:
  0.0 163.9 jit_solution(10801642832779018770)
XLA Ops:
  0.0 0.0 copy-start
  0.0 1.1 multiply_reduce_fusion.1
  1.2 0.7 convert_bitcast_fusion
  1.8 0.6 pad_add_fusion.at_ref
  2.5 0.1 broadcast_in_dim.139
  2.5 0.1 broadcast_in_dim.140
  2.6 0.1 copy.32
  2.7 0.7 dynamic-slice_bitcast_fusion
  3.4 0.7 constant_dynamic-slice_fusion
  4.1 0.8 fusion.26
  4.9 0.1 broadcast_select_fusion
  5.0 1.5 pad_maximum_fusion.x_ref
  6.5 0.1 mul.141
  6.7 17.7 %enter.1 = (bf16[4,8,1152]{2,1,0:T(8,128)(2,1)}, bf16[4,2,4,8,1152]{4,3,2,1,0:T(8,128)(2,1)}) custom-call(bf16[4,8,1152]{2,1,0:T(8,128)(2,1)} %pad_maximum_fusion.x_ref), custom_call_target="tpu_custom_call" | custom-call | tf_op jit(solution)/shard_map/enter/pallas_call | solution.py:97
  24.4 0.9 slice_convert_fusion
  25.2 0.6 compare_reduce_fusion
  25.9 0.7 eq.51
  26.5 0.2 fusion.24
  26.8 1.3 select_convert_fusion.1
  28.1 0.2 fusion.22
  28.4 0.1 eq.57
  28.4 0.0 copy-done
  28.5 0.7 fusion.15
  29.2 0.4 concatenate.10
  29.6 0.1 copy.28
  29.6 0.9 maximum_bitcast_fusion.refs_0_
  30.5 10.2 %reduce_1_dp.1 = f32[80,512]{1,0:T(8,128)} custom-call(bf16[4,2,80,512]{3,2,1,0:T(8,128)(2,1)} %maximum_bitcast_fusion.refs_0_), custom_call_target="tpu_custom_call" | custom-call | tf_op jit(solution)/shard_map/reduce_1_dp/pallas_call | solution.py:97
  40.8 0.7 slice.43
  41.5 0.7 slice.42
  42.2 0.9 slice.41
  43.2 0.1 multiply_reduce_fusion
  43.4 0.2 multiply_bitcast_fusion
  43.6 0.1 mul.139
  43.8 0.2 mul.140
  44.0 0.7 broadcast_multiply_fusion.q_ref
  44.7 13.9 %attend.1.x_ref = bf16[64,512]{1,0:T(8,128)(2,1)} custom-call(s32[2]{0:T(128)} %pad_add_fusion.at_ref, bf16[2,256,256]{2,1,0:T(8,128)(2,1)} %broadcast_multiply_fusion.q_ref, bf16[8192,1024]{1,0:T(8,128)(2,1)} %bitcast.76, bf16[8192,1024]{1,0:T(8,128)(2,1)} %bitcast.77, s32[1,8192]{1,0:T(1,128)} %m_ref.1), custom_call_target="tpu_custom_call" | custom-call | tf_op jit(solution)/shard_map/attend/pallas_call | solution.py:423
  58.6 9.1 %gather_2_dp.1 = bf16[4,64,1024]{2,1,0:T(8,128)(2,1)} custom-call(bf16[64,512]{1,0:T(8,128)(2,1)} %attend.1.x_ref), custom_call_target="tpu_custom_call" | custom-call | tf_op jit(solution)/shard_map/gather_2_dp/pallas_call | solution.py:97
  67.6 0.0 copy-done.2
  67.7 2.5 %fusion.18 = bf16[256,1024]{1,0:T(8,128)(2,1)} fusion(bf16[256,1024]{1,0:T(8,128)(2,1)} %bitcast.87, bf16[1,1024,1024]{2,1,0:T(8,128)(2,1)S(1)} %copy-done.3, pred[256]{0:T(512)(128)(4,1)S(1)} %copy-done.2), kind=kOutput, calls=%fused_computation.10 | convolution fusion | flops 537395200 | bytes 3145984 | tf_op jit(solution)/shard_map/dot_general | solution.py:574
  70.2 20.6 %renew.1 = (f32[4,8,1024]{2,1,0:T(8,128)}, bf16[4,2,4,8,1152]{4,3,2,1,0:T(8,128)(2,1)}) custom-call(bf16[4,2,4,8,1024]{4,3,2,1,0:T(8,128)(2,1)} %bitcast.86, bf16[4,8,1152]{2,1,0:T(8,128)(2,1)} %get-tuple-element.12.own_ref), custom_call_target="tpu_custom_call" | custom-call | tf_op jit(solution)/shard_map/renew/pallas_call | solution.py:97
  90.8 1.6 select_bitcast_fusion.tag_ref
  92.4 2.0 %select_convert_fusion = bf16[4,2,4,8,1024]{4,3,2,1,0:T(8,128)(2,1)} fusion(f32[1024]{0:T(1024)S(1)} %bitcast.95, bf16[4,2,4,8,1152]{4,3,2,1,0:T(8,128)(2,1)} %get-tuple-element.13, pred[4,2,4,8]{3,2,1,0:T(4,128)(4,1)S(1)} %compare_reduce_fusion), kind=kLoop, calls=%fused_computation.11 | loop fusion | flops 1048576 | bytes 1052928 | tf_op jit(solution)/shard_map/convert_element_type | solution.py:582
  94.4 9.0 %expand.1 = (bf16[256,2752]{1,0:T(8,128)(2,1)}, bf16[256,2752]{1,0:T(8,128)(2,1)}) custom-call(bf16[256,1024]{1,0:T(8,128)(2,1)} %bitcast.80, bf16[2752,1024]{1,0:T(8,128)(2,1)} %bitcast.78, bf16[2752,1024]{1,0:T(8,128)(2,1)} %bitcast.79), custom_call_target="tpu_custom_call" | custom-call | tf_op jit(solution)/shard_map/expand/pallas_call | solution.py:313
  103.4 36.0 %activate.1 = bf16[4,2,32,2752]{3,2,1,0:T(8,128)(2,1)} custom-call(bf16[4,2,32,2752]{3,2,1,0:T(8,128)(2,1)} %bitcast.81, bf16[4,2,32,2752]{3,2,1,0:T(8,128)(2,1)} %bitcast.82, bf16[4,2,32,128]{3,2,1,0:T(8,128)(2,1)} %select_bitcast_fusion.tag_ref), custom_call_target="tpu_custom_call" | custom-call | tf_op jit(solution)/shard_map/activate/pallas_call | solution.py:97
  139.4 0.0 copy-start.1
  139.4 5.6 %fusion.12 = bf16[256,1024]{1,0:T(8,128)(2,1)} fusion(bf16[256,2752]{1,0:T(8,128)(2,1)} %bitcast.83, bf16[1,2752,1024]{2,1,0:T(8,128)(2,1)} %param.27, pred[256]{0:T(512)(128)(4,1)S(1)} %copy-done.2), kind=kOutput, calls=%fused_computation.8 | convolution fusion | flops 1443364864 | bytes 7569664 | tf_op jit(solution)/shard_map/dot_general | solution.py:574
  145.1 17.4 %leave.1 = bf16[8,4096]{1,0:T(8,128)(2,1)} custom-call(bf16[4,2,4,8,1024]{4,3,2,1,0:T(8,128)(2,1)} %bitcast.89, f32[4,8,1024]{2,1,0:T(8,128)} %get-tuple-element.16.residual_ref), custom_call_target="tpu_custom_call" | custom-call | tf_op jit(solution)/shard_map/leave/pallas_call | solution.py:97
  162.5 1.5 copy.41
  (24 shorter events, 0.2 us)
Async XLA Ops:
  0.0 28.4 %copy-start = (bf16[1,1024,1024]{2,1,0:T(8,128)(2,1)S(1)}, bf16[1,1024,1024]{2,1,0:T(8,128)(2,1)}, u32[]{:S(2)}) copy-start(bf16[1,1024,1024]{2,1,0:T(8,128)(2,1)} %param.20) | copy-start | bytes 6291460
  44.7 23.0 %copy-start.2 = (pred[256]{0:T(512)(128)(4,1)S(1)}, pred[256]{0:T(512)(128)(4,1)}, u32[]{:S(2)}) copy-start(pred[256]{0:T(512)(128)(4,1)} %eq.51) | copy-start | bytes 772
  44.7 23.0 %copy-start.3 = (bf16[1,1024,1024]{2,1,0:T(8,128)(2,1)S(1)}, bf16[1,1024,1024]{2,1,0:T(8,128)(2,1)}, u32[]{:S(2)}) copy-start(bf16[1,1024,1024]{2,1,0:T(8,128)(2,1)} %param.23) | copy-start | bytes 6291460
  139.4 24.5 %copy-start.1 = (bf16[1,1024,1024]{2,1,0:T(8,128)(2,1)S(1)}, bf16[1,1024,1024]{2,1,0:T(8,128)(2,1)}, u32[]{:S(2)}) copy-start(bf16[1,1024,1024]{2,1,0:T(8,128)(2,1)} %param.20) | copy-start | bytes 6291460
